TPU v7x, 128 devices: a whole 4x4x4 slice. The times are simulated.
128 devices in a mesh: gx: 16 (over x_lo, z, core), gy: 8 (over y, x_hi).
Axes of the slice: x: 4 (x_hi: 2, x_lo: 2; x = x_hi * 2 + x_lo), y: 4, z: 4, core: 2. Of those that a mesh axis runs over, the one named last changes fastest.
Arguments:
- electric: float32 [3, 16, 1024, 2048], P(None, None, 'gx', 'gy'), may hold values from -6 to 6
- magnetic: float32 [3, 16, 1024, 2048], P(None, None, 'gx', 'gy'), may hold values from -6 to 6
- inverse_permittivity: float32 [3, 16, 1024, 2048], P(None, None, 'gx', 'gy'), may hold values from 0.1 to 1
- forward_spectrum: float32 [4, 2, 3, 4, 1024, 2048], P(None, None, None, None, 'gx', 'gy'), may hold values from -6 to 6
- frequencies: float32 [4], replicated, may hold values from 0.3 to 1.2
- design_mask: int32 [4, 1024, 2048], P(None, 'gx', 'gy'), may hold values 0 or 1
- row_owner: int32 [1024, 1], replicated, may hold values from 0 to 15; in each aligned block of 64 rows (0 to 63, 64 to 127, ...) at most 8 rows name the same one
Outputs:
- electric_out: float32 [3, 16, 1024, 2048], P(None, None, 'gx', 'gy')
- magnetic_out: float32 [3, 16, 1024, 2048], P(None, None, 'gx', 'gy')
- owned_gradient: float32 [4, 4, 2048, 2048], P(None, None, 'gx', 'gy')
Inputs may be any that keep to these rules, and one draw needn't show every extreme that they name: `row_owner`: in each aligned block of 64 rows (the rows of one tile along gx) no owner is named by more than 8 rows; in some block an owner is named by exactly 8 rows.
All inputs are finite; a program needn't handle non-finite values. No bound on the sum of `design_mask` on one device may be relied on, other than what follows from the above.
Results may differ from a plain program's by a relative error of at most 0.0003.
Values sent between devices are 32-bit elements; how exact they have to be, the bound alone decides.
A program may use at most 128 MiB of HBM per device.

v0:
```python
import math

import jax
import jax.numpy as jnp
from jax import lax
from jax.sharding import PartitionSpec as P

DP = 4
FREQ = 4
STEPS = 3
RADIUS = 3


COURANT = 0.5


def shifted(value, axis, steps):
    count = lax.axis_size(axis)
    leading, last = (max(0, -steps), min(count, count - steps))
    return lax.ppermute(value, axis, [(source, source + steps) for source in range(leading, last)])


def padded(block, sides, width):
    for axis, dim in sides:
        count = lax.axis_size(axis)
        forward = [(i, i + 1) for i in range(count - 1)]
        backward = [(target, source) for source, target in forward]
        low = lax.ppermute(
            lax.slice_in_dim(block, block.shape[dim] - width, None, axis=dim), axis, forward
        )
        high = lax.ppermute(lax.slice_in_dim(block, 0, width, axis=dim), axis, backward)
        block = jnp.concatenate([low, block, high], axis=dim)
    return block


def filter_table():
    table = []
    for shift_x in range(-RADIUS, RADIUS + 1):
        for shift_y in range(-RADIUS, RADIUS + 1):
            weight = RADIUS + 1.0 - math.sqrt(shift_x * shift_x + shift_y * shift_y)
            if weight > 0.0:
                table.append((shift_x, shift_y, weight))
    return table


def across_x(piece, offset):
    return shifted(piece, "gx", offset)


def across_y(piece, offset):
    return shifted(piece, "gy", offset)


def plus_x(field, layer):
    return jnp.concatenate([field[:, 1:, :], layer[:, None, :]], axis=1) - field


def plus_y(field, layer):
    return jnp.concatenate([field[:, :, 1:], layer[:, :, None]], axis=2) - field


def plus_z(field):
    return jnp.concatenate([field[1:], jnp.zeros_like(field[:1])], axis=0) - field


def minus_x(field, layer):
    return field - jnp.concatenate([layer[:, None, :], field[:, :-1, :]], axis=1)


def minus_y(field, layer):
    return field - jnp.concatenate([layer[:, :, None], field[:, :, :-1]], axis=2)


def minus_z(field):
    return field - jnp.concatenate([jnp.zeros_like(field[:1]), field[:-1]], axis=0)


def advance(electric, magnetic, inverse):
    depth, rows, cols = (electric.shape[1], electric.shape[2], electric.shape[3])
    elec_x, elec_y, elec_z = (electric[0], electric[1], electric[2])
    upper_x = across_x(
        jnp.stack([elec_y[:, 0, :], elec_z[:, 0, :]]).reshape(2, depth * cols), -1
    ).reshape(2, depth, cols)
    upper_y = across_y(
        jnp.stack([elec_x[:, :, 0], elec_z[:, :, 0]]).reshape(2, depth * rows), -1
    ).reshape(2, depth, rows)
    magn_x = magnetic[0] - COURANT * (plus_y(elec_z, upper_y[1]) - plus_z(elec_y))
    magn_y = magnetic[1] - COURANT * (plus_z(elec_x) - plus_x(elec_z, upper_x[1]))
    magn_z = magnetic[2] - COURANT * (plus_x(elec_y, upper_x[0]) - plus_y(elec_x, upper_y[0]))
    lower_x = across_x(
        jnp.stack([magn_y[:, rows - 1, :], magn_z[:, rows - 1, :]]).reshape(2, depth * cols), 1
    ).reshape(2, depth, cols)
    lower_y = across_y(
        jnp.stack([magn_x[:, :, cols - 1], magn_z[:, :, cols - 1]]).reshape(2, depth * rows), 1
    ).reshape(2, depth, rows)
    elec_x = elec_x + COURANT * inverse[0] * (minus_y(magn_z, lower_y[1]) - minus_z(magn_y))
    elec_y = elec_y + COURANT * inverse[1] * (minus_z(magn_x) - minus_x(magn_z, lower_x[1]))
    elec_z = elec_z + COURANT * inverse[2] * (
        minus_x(magn_y, lower_x[0]) - minus_y(magn_x, lower_y[0])
    )
    return (jnp.stack([elec_x, elec_y, elec_z]), jnp.stack([magn_x, magn_y, magn_z]))


def spectral_term(design, forward_spectrum, frequencies, count):
    phase = frequencies * (count + 1.0)
    cosine = jnp.cos(phase)
    sine = jnp.sin(phase)
    terms = []
    for freq in range(FREQ):
        weight = forward_spectrum[freq, 0] * cosine[freq] + forward_spectrum[freq, 1] * sine[freq]
        terms.append(jnp.sum(weight * design, axis=0))
    return jnp.stack(terms)


def body(
    electric, magnetic, inverse_permittivity, forward_spectrum, frequencies, design_mask, row_owner
):
    depth, rows, cols = (electric.shape[1], electric.shape[2], electric.shape[3])
    first = (depth - DP) // 2
    tiles_x = lax.axis_size("gx")
    tiles_y = lax.axis_size("gy")
    index_x = lax.axis_index("gx")
    index_y = lax.axis_index("gy")
    raw = jnp.zeros((FREQ, DP, rows, cols), jnp.float32)
    for count in range(STEPS):
        electric, magnetic = advance(electric, magnetic, inverse_permittivity)
        design = electric[:, first : first + DP]
        raw = raw + spectral_term(design, forward_spectrum, frequencies, count)
    masked = raw * design_mask.astype(jnp.float32)[None]
    extended = padded(masked, (("gx", 2), ("gy", 3)), RADIUS)
    global_x = index_x * rows + jnp.arange(rows, dtype=jnp.int32)
    global_y = index_y * cols + jnp.arange(cols, dtype=jnp.int32)
    total = jnp.zeros_like(masked)
    normal = jnp.zeros((rows, cols), jnp.float32)
    for shift_x, shift_y, weight in filter_table():
        total = (
            total
            + weight
            * extended[
                :,
                :,
                RADIUS + shift_x : RADIUS + shift_x + rows,
                RADIUS + shift_y : RADIUS + shift_y + cols,
            ]
        )
        inside_x = ((global_x + shift_x >= 0) & (global_x + shift_x < rows * tiles_x)).astype(
            jnp.float32
        )
        inside_y = ((global_y + shift_y >= 0) & (global_y + shift_y < cols * tiles_y)).astype(
            jnp.float32
        )
        normal = normal + weight * (inside_x[:, None] * inside_y[None, :])
    filtered = total / normal
    capacity = max(2, 2 * rows // tiles_x)
    slot_count = tiles_x * capacity
    owners = row_owner[:, 0]
    onehot = (owners[:, None] == jnp.arange(tiles_x, dtype=jnp.int32)[None, :]).astype(jnp.int32)
    blocks = onehot.reshape(tiles_x, rows, tiles_x)
    before = jnp.cumsum(blocks, axis=1) - blocks
    position = jnp.sum(before * blocks, axis=2).reshape(tiles_x * rows)
    tiles = jnp.arange(tiles_x * rows, dtype=jnp.int32) // rows
    slot_ids = jnp.arange(slot_count, dtype=jnp.int32)
    wanted_all = jnp.where(owners == index_x, tiles * capacity + position, -1)
    picker = (wanted_all[None, :] == slot_ids[:, None]).astype(jnp.float32)
    owned = jnp.einsum(
        "sr,fprc->fpsc",
        picker,
        lax.all_gather(filtered, "gx", axis=2, tiled=True),
        precision=lax.Precision.HIGHEST,
    )
    return (electric, magnetic, owned)


def solution(mesh):
    placed = (
        P(None, None, "gx", "gy"),
        P(None, None, "gx", "gy"),
        P(None, None, "gx", "gy"),
        P(None, None, None, None, "gx", "gy"),
        P(),
        P(None, "gx", "gy"),
        P(),
    )
    return jax.shard_map(
        body,
        mesh=mesh,
        in_specs=placed,
        out_specs=(P(None, None, "gx", "gy"), P(None, None, "gx", "gy"), P(None, None, "gx", "gy")),
        check_vma=False,
    )
```

profile of v0, /device:TPU:1, one launch (start us, length us, event | category | flops | bytes accessed | tf_op | source)
XLA Modules:
  0.0 358.3 jit_solution(14583949485658786114)
XLA Ops:
  7.2 3.3 slice_bitcast_fusion.2
  12.1 1.3 collective-permute-start.1
  15.2 3.3 collective-permute-start
  18.7 1.4 slice_bitcast_fusion.4
  22.2 1.1 slice.804
  23.3 1.3 slice.808
  24.6 1.1 slice.818
  25.7 1.3 slice.812
  27.8 1.1 broadcast_in_dim_squeeze.97
  28.9 1.1 broadcast_in_dim_squeeze.96
  30.1 6.5 %fusion.58 = (f32[16,64,256]{2,1,0:T(8,128)S(1)}, f32[16,64,256]{2,1,0:T(8,128)S(1)}, f32[16,64,256]{2,1,0:T(8,128)}) fusion(f32[16,64,1]{2,1,0:T(8,128)} %broadcast_in_dim_squeeze.97, f32[16,64,255]{2,1,0:T(8,128)} %slice.812, f32[15,64,256]{2,1,0:T(8,128)} %get-tuple-element.51, f32[3,16,64,256]{3,2,1,0:T(8,128)} %param.8, ...), kind=kLoop, calls=%fused_computation.113 | loop fusion | flops 4980736 | bytes 15597568 | tf_op jit(solution)/shard_map/sub | solution.py:87
  39.4 5.8 %collective-permute-start.2 = (f32[2,1024]{1,0:T(2,128)S(1)}, f32[2,1024]{1,0:T(2,128)S(1)}, u32[]{:S(2)}, u32[]{:S(2)}) collective-permute-start(f32[2,1024]{1,0:T(2,128)S(1)} %pad_maximum_fusion.17), channel_id=1, source_target_pairs={{0,1},{1,2},{2,3},{3,4},{4,5},{5,6},{6,7},{8,9},{9,10},{10,11},{11... | collective-permute-start | bytes 24584 | tf_op jit(solution)/shard_map/ppermute | solution.py:20
  45.2 2.2 slice.821
  48.5 3.8 %collective-permute-start.3 = (f32[2,4096]{1,0:T(2,128)S(1)}, f32[2,4096]{1,0:T(2,128)S(1)}, u32[]{:S(2)}, u32[]{:S(2)}) collective-permute-start(f32[2,4096]{1,0:T(2,128)S(1)} %pad_maximum_fusion.11), channel_id=1, source_target_pairs={{0,8},{8,16},{16,24},{24,32},{32,40},{40,48},{48,56},{56,64},{64,7... | collective-permute-start | bytes 98312 | tf_op jit(solution)/shard_map/ppermute | solution.py:20
  52.4 1.1 broadcast_in_dim_squeeze.98
  53.5 1.2 broadcast_in_dim_squeeze.99
  54.7 7.3 %fusion.61 = (f32[16,64,256]{2,1,0:T(8,128)S(1)}, f32[16,64,256]{2,1,0:T(8,128)S(1)}, f32[16,64,256]{2,1,0:T(8,128)S(1)}) fusion(f32[16,64,256]{2,1,0:T(8,128)} %copy-done.5, f32[16,64,255]{2,1,0:T(8,128)} %bitcast.200, f32[16,64,1]{2,1,0:T(8,128)} %broadcast_in_dim_squeeze.98, f32[16,64,256]{2,1,0:T(8,128)} %get-tuple-element.44, ...), kind=kLoop, calls=%fused_computation.117 | loop fusion | flops 5767168 | bytes 18743296 | tf_op jit(solution)/shard_map/add | solution.py:96
  62.7 1.3 collective-permute-start.5
  64.0 9.7 %fusion.123 = (f32[4,64,256]{2,1,0:T(8,128)S(1)}, f32[4,64,256]{2,1,0:T(8,128)}, f32[4,64,256]{2,1,0:T(8,128)}, f32[4,64,256]{2,1,0:T(8,128)}) fusion(f32[4,2,3,4,64,256]{5,4,3,2,1,0:T(8,128)} %param.10, f32[]{:T(128)} %bitcast.42, f32[]{:T(128)} %bitcast.41, f32[]{:T(128)} %bitcast.53, f32[]{:T(128)} %bitcast.52, f32[]{:T(128)} %bitcast.49, f32[]{:T(128)} %bitcast.48, ...), kind=kLoop, calls=%fused_computation.224 | loop fusion | flops 4063232 | bytes 10485792 | tf_op jit(solution)/shard_map/reduce_sum | solution.py:111
  74.8 1.1 slice.840
  75.8 1.3 slice.834
  77.2 1.1 slice.826
  78.3 1.1 slice.846
  79.4 1.3 slice.838
  80.7 2.2 collective-permute-start.4
  82.9 1.2 broadcast_in_dim_squeeze.101
  84.1 1.2 broadcast_in_dim_squeeze.100
  86.0 6.4 %fusion.76 = (f32[16,64,256]{2,1,0:T(8,128)S(1)}, f32[16,64,256]{2,1,0:T(8,128)S(1)}, f32[16,64,256]{2,1,0:T(8,128)}) fusion(f32[16,64,256]{2,1,0:T(8,128)} %copy-done.9, f32[16,64,256]{2,1,0:T(8,128)S(1)} %get-tuple-element.40, f32[16,64,1]{2,1,0:T(8,128)} %broadcast_in_dim_squeeze.101, f32[16,64,255]{2,1,0:T(8,128)} %slice.838, ...), kind=kLoop, calls=%fused_computation.139 | loop fusion | flops 4980736 | bytes 15597568 | tf_op jit(solution)/shard_map/sub | solution.py:87
  95.3 6.2 %collective-permute-start.6 = (f32[2,1024]{1,0:T(2,128)S(1)}, f32[2,1024]{1,0:T(2,128)S(1)}, u32[]{:S(2)}, u32[]{:S(2)}) collective-permute-start(f32[2,1024]{1,0:T(2,128)S(1)} %pad_maximum_fusion.19), channel_id=1, source_target_pairs={{0,1},{1,2},{2,3},{3,4},{4,5},{5,6},{6,7},{8,9},{9,10},{10,11},{11... | collective-permute-start | bytes 24584 | tf_op jit(solution)/shard_map/ppermute | solution.py:20
  101.5 2.2 slice.849
  104.9 3.3 collective-permute-start.7
  108.2 1.1 broadcast_in_dim_squeeze.102
  109.3 1.1 broadcast_in_dim_squeeze.103
  110.5 8.5 %fusion.79 = (f32[16,64,256]{2,1,0:T(8,128)S(1)}, f32[16,64,256]{2,1,0:T(8,128)S(1)}, f32[16,64,256]{2,1,0:T(8,128)}) fusion(f32[16,64,256]{2,1,0:T(8,128)} %copy-done, f32[16,64,256]{2,1,0:T(8,128)} %copy-done.4, f32[16,64,255]{2,1,0:T(8,128)} %bitcast.198, f32[16,64,1]{2,1,0:T(8,128)} %broadcast_in_dim_squeeze.102, f32[16,64,256]{2,1,0:T(8,128)} %get-tuple-element.67, ...), kind=kLoop, calls=%fused_computation.143 | loop fusion | flops 5767168 | bytes 18743296 | tf_op jit(solution)/shard_map/add | solution.py:96
  120.5 1.3 collective-permute-start.9
  121.9 9.7 %fusion.119 = (f32[4,64,256]{2,1,0:T(8,128)}, f32[4,64,256]{2,1,0:T(8,128)}, f32[4,64,256]{2,1,0:T(8,128)}, f32[4,64,256]{2,1,0:T(8,128)}) fusion(f32[4,2,3,4,64,256]{5,4,3,2,1,0:T(8,128)} %param.10, f32[]{:T(128)} %bitcast.61, f32[]{:T(128)} %bitcast.60, f32[]{:T(128)} %bitcast.72, f32[]{:T(128)} %bitcast.71, f32[]{:T(128)} %bitcast.68, f32[]{:T(128)} %bitcast.67, ...), kind=kLoop, calls=%fused_computation.216 | loop fusion | flops 4063232 | bytes 10485792 | tf_op jit(solution)/shard_map/reduce_sum | solution.py:111
  131.6 1.1 slice.873
  133.7 1.3 slice.862
  135.1 1.1 slice.854
  136.2 1.1 slice.874
  137.3 1.3 slice.866
  138.6 1.9 collective-permute-start.8
  140.5 1.2 broadcast_in_dim_squeeze.105
  141.7 1.1 broadcast_in_dim_squeeze.104
  143.8 6.4 %fusion.94 = (f32[16,64,256]{2,1,0:T(8,128)S(1)}, f32[16,64,256]{2,1,0:T(8,128)S(1)}, f32[16,64,256]{2,1,0:T(8,128)}) fusion(f32[16,64,256]{2,1,0:T(8,128)} %copy-done.8, f32[16,64,256]{2,1,0:T(8,128)S(1)} %get-tuple-element.49, f32[16,64,1]{2,1,0:T(8,128)} %broadcast_in_dim_squeeze.105, f32[16,64,255]{2,1,0:T(8,128)} %slice.866, ...), kind=kLoop, calls=%fused_computation.165 | loop fusion | flops 4980736 | bytes 15597568 | tf_op jit(solution)/shard_map/sub | solution.py:87
  153.1 6.4 %collective-permute-start.10 = (f32[2,1024]{1,0:T(2,128)S(1)}, f32[2,1024]{1,0:T(2,128)S(1)}, u32[]{:S(2)}, u32[]{:S(2)}) collective-permute-start(f32[2,1024]{1,0:T(2,128)S(1)} %pad_maximum_fusion.21), channel_id=1, source_target_pairs={{0,1},{1,2},{2,3},{3,4},{4,5},{5,6},{6,7},{8,9},{9,10},{10,11},{11... | collective-permute-start | bytes 24584 | tf_op jit(solution)/shard_map/ppermute | solution.py:20
  159.6 2.2 slice.877
  161.8 2.2 slice.876
  164.0 15.2 %collective-permute-start.11 = (f32[2,4096]{1,0:T(2,128)S(1)}, f32[2,4096]{1,0:T(2,128)S(1)}, u32[]{:S(2)}, u32[]{:S(2)}) collective-permute-start(f32[2,4096]{1,0:T(2,128)S(1)} %pad_maximum_fusion.15), channel_id=1, source_target_pairs={{0,8},{8,16},{16,24},{24,32},{32,40},{40,48},{48,56},{56,64},{64,7... | collective-permute-start | bytes 98312 | tf_op jit(solution)/shard_map/ppermute | solution.py:20
  179.3 1.1 broadcast_in_dim_squeeze.106
  180.5 1.1 broadcast_in_dim_squeeze.107
  181.7 6.9 %fusion.98 = (f32[1,16,64,256]{3,2,1,0:T(8,128)S(1)}, f32[1,16,64,256]{3,2,1,0:T(8,128)S(1)}, f32[1,16,64,256]{3,2,1,0:T(8,128)S(1)}) fusion(f32[16,64,256]{2,1,0:T(8,128)S(1)} %get-tuple-element.48, f32[16,64,256]{2,1,0:T(8,128)} %copy-done.6, f32[16,64,255]{2,1,0:T(8,128)} %bitcast.202, f32[16,64,1]{2,1,0:T(8,128)} %broadcast_in_dim_squeeze.106, ...), kind=kLoop, calls=%fused_computation.170 | loop fusion | flops 5767168 | bytes 18743296 | tf_op jit(solution)/shard_map/stack | solution.py:101
  189.1 6.9 %fusion.115 = (f32[4,64,256]{2,1,0:T(8,128)S(1)}, f32[4,64,256]{2,1,0:T(8,128)S(1)}, f32[4,64,256]{2,1,0:T(8,128)S(1)}, f32[4,64,256]{2,1,0:T(8,128)S(1)}) fusion(f32[4,2,3,4,64,256]{5,4,3,2,1,0:T(8,128)S(1)} %bitcast.191, f32[3,16,64,256]{3,2,1,0:T(8,128)S(1)} %pad_maximum_fusion, f32[]{:T(128)} %bitcast.80, f32[]{:T(128)} %bitcast.79, f32[]{:T(128)} %bitcast.84, ...), kind=kLoop, calls=%fused_computation.208 | loop fusion | flops 3670016 | bytes 8126496 | tf_op jit(solution)/shard_map/reduce_sum | solution.py:111
  196.4 2.9 collective-permute-start.12
  199.3 1.9 collective-permute-start.13
  201.3 3.6 %collective-permute-done.13 = f32[4,4,3,256]{3,2,1,0:T(4,128)S(1)} collective-permute-done((f32[4,4,3,256]{3,2,1,0:T(4,128)S(1)}, f32[4,4,3,256]{3,2,1,0:T(4,128)S(1)}, u32[]{:S(2)}, u32[]{:S(2)}) %collective-permute-start.13) | collective-permute-done | bytes 49184 | tf_op jit(solution)/shard_map/ppermute | solution.py:31
  205.8 1.3 collective-permute-start.15
  207.1 6.4 %collective-permute-start.14 = (f32[4,4,70,3]{2,1,3,0:T(4,128)S(1)}, f32[4,4,70,3]{2,1,3,0:T(4,128)S(1)}, u32[]{:S(2)}, u32[]{:S(2)}) collective-permute-start(f32[4,4,70,3]{2,1,3,0:T(4,128)S(1)} %copy.56), channel_id=1, source_target_pairs={{0,1},{1,2},{2,3},{3,4},{4,5},{5,6},{6,7},{8,9},{9,10},{10,11},{11... | collective-permute-start | bytes 40328 | tf_op jit(solution)/shard_map/ppermute | solution.py:28
  215.9 12.5 %fusion.11 = f32[4,4,64,256]{3,2,1,0:T(8,128)} fusion(f32[4,4,64,256]{3,2,1,0:T(8,128)} %copy-done.15, f32[4,4,3,256]{3,2,1,0:T(4,128)S(1)} %collective-permute-done.13, f32[4,4,3,256]{3,2,1,0:T(4,128)S(1)} %collective-permute-done.12, f32[4,4,70,259]{3,2,1,0:T(8,128)S(1)} %get-tuple-element.57, f32[4,4,70,259]{3,2,1,0:T(8,128)S(1)} %get-tuple-element.56, ...), kind=kLoop, calls=%fused_computation.25 | loop fusion | flops 24117248 | bytes 42106880 | tf_op jit(solution)/shard_map/div | solution.py:153
  229.7 1.4 select_reduce_fusion
  231.4 1.9 pad_maximum_fusion.1
  233.3 99.4 %all-gather.2.cloned.1.call-done = f32[4,4,1024,256]{3,2,1,0:T(8,128)} async-done(((f32[4,4,64,256]{3,2,1,0:T(8,128)}), f32[4,4,1024,256]{3,2,1,0:T(8,128)}) %all-gather.2.cloned.1.call-update) | async-done | bytes 16777232 | tf_op jit(solution)/shard_map/all_gather | solution.py:168
  332.7 16.8 %convolution_bitcast_fusion = f32[4,4,128,256]{2,3,1,0:T(8,128)S(1)} fusion(f32[4,4,1024,256]{3,2,1,0:T(8,128)} %all-gather.2.cloned.1.call-done, s32[1024]{0:T(1024)S(1)} %fusion.134), kind=kOutput, calls=%fused_computation.8 | convolution fusion | flops 6442582016 | bytes 18878464 | tf_op jit(solution)/shard_map/sr,fprc->fpsc/dot_general | solution.py:165
  349.5 1.8 copy.62
  (183 shorter events, 28.5 us)
Async XLA Ops:
  7.2 11.5 %copy-start.1 = (f32[3,16,64,256]{3,2,1,0:T(8,128)S(1)}, f32[3,16,64,256]{3,2,1,0:T(8,128)}, u32[]{:S(2)}) copy-start(f32[3,16,64,256]{3,2,1,0:T(8,128)} %param.7) | copy-start | bytes 9437188
  7.2 325.5 %all-gather.2.cloned.1.call-start = ((), (), s32[]{:S(2)}) async-start(), calls=%async_computation | async-start | bytes 17825792 | tf_op jit(solution)/shard_map/all_gather | solution.py:168
  10.6 1.0 copy-start.16
  10.6 1.3 copy-start.18
  10.6 9.6 %copy-start.32 = (f32[4]{0:T(128)S(1)}, f32[4]{0:T(128)}, u32[]{:S(2)}) copy-start(f32[4]{0:T(128)} %param.11) | copy-start | bytes 52
  12.1 15.7 %collective-permute-start.1 = (f32[2,1024]{1,0:T(2,128)S(1)}, f32[2,1024]{1,0:T(2,128)S(1)}, u32[]{:S(2)}, u32[]{:S(2)}) collective-permute-start(f32[2,1024]{1,0:T(2,128)S(1)} %pad_maximum_fusion.16), channel_id=1, source_target_pairs={{1,0},{2,1},{3,2},{4,3},{5,4},{6,5},{7,6},{9,8},{10,9},{11,10},{12... | collective-permute-start | bytes 24584 | tf_op jit(solution)/shard_map/ppermute | solution.py:20
  15.2 14.8 %collective-permute-start = (f32[2,4096]{1,0:T(2,128)S(1)}, f32[2,4096]{1,0:T(2,128)S(1)}, u32[]{:S(2)}, u32[]{:S(2)}) collective-permute-start(f32[2,4096]{1,0:T(2,128)S(1)} %pad_maximum_fusion.10), channel_id=1, source_target_pairs={{8,0},{16,8},{24,16},{32,24},{40,32},{48,40},{56,48},{64,56},{72,6... | collective-permute-start | bytes 98312 | tf_op jit(solution)/shard_map/ppermute | solution.py:20
  18.6 3.6 %copy-start.21 = (f32[16,64,256]{2,1,0:T(8,128)S(1)}, f32[16,64,256]{2,1,0:T(8,128)}, u32[]{:S(2)}) copy-start(f32[16,64,256]{2,1,0:T(8,128)} %get-tuple-element.55) | copy-start | bytes 3145732
  18.6 4.7 %copy-start.19 = (f32[16,64,256]{2,1,0:T(8,128)S(1)}, f32[16,64,256]{2,1,0:T(8,128)}, u32[]{:S(2)}) copy-start(f32[16,64,256]{2,1,0:T(8,128)} %copy-done.18) | copy-start | bytes 3145732
  18.7 5.9 %copy-start.17 = (f32[16,64,256]{2,1,0:T(8,128)S(1)}, f32[16,64,256]{2,1,0:T(8,128)}, u32[]{:S(2)}) copy-start(f32[16,64,256]{2,1,0:T(8,128)} %copy-done.16) | copy-start | bytes 3145732
  23.3 3.7 %copy-start.30 = (s32[4,64,256]{2,1,0:T(8,128)S(1)}, s32[4,64,256]{2,1,0:T(8,128)}, u32[]{:S(2)}) copy-start(s32[4,64,256]{2,1,0:T(8,128)} %param.12) | copy-start | bytes 786436
  36.6 1.0 copy-start.5
  36.6 1.3 copy-start.9
  36.6 10.9 %copy-start.13 = (f32[16,64,256]{2,1,0:T(8,128)S(1)}, f32[16,64,256]{2,1,0:T(8,128)}, u32[]{:S(2)}) copy-start(f32[16,64,256]{2,1,0:T(8,128)} %get-tuple-element.44) | copy-start | bytes 3145732
  39.4 12.9 %collective-permute-start.2 = (f32[2,1024]{1,0:T(2,128)S(1)}, f32[2,1024]{1,0:T(2,128)S(1)}, u32[]{:S(2)}, u32[]{:S(2)}) collective-permute-start(f32[2,1024]{1,0:T(2,128)S(1)} %pad_maximum_fusion.17), channel_id=1, source_target_pairs={{0,1},{1,2},{2,3},{3,4},{4,5},{5,6},{6,7},{8,9},{9,10},{10,11},{11... | collective-permute-start | bytes 24584 | tf_op jit(solution)/shard_map/ppermute | solution.py:20
  48.5 6.1 %collective-permute-start.3 = (f32[2,4096]{1,0:T(2,128)S(1)}, f32[2,4096]{1,0:T(2,128)S(1)}, u32[]{:S(2)}, u32[]{:S(2)}) collective-permute-start(f32[2,4096]{1,0:T(2,128)S(1)} %pad_maximum_fusion.11), channel_id=1, source_target_pairs={{0,8},{8,16},{16,24},{24,32},{32,40},{40,48},{48,56},{56,64},{64,7... | collective-permute-start | bytes 98312 | tf_op jit(solution)/shard_map/ppermute | solution.py:20
  62.0 24.0 %copy-start = (f32[16,64,256]{2,1,0:T(8,128)}, f32[16,64,256]{2,1,0:T(8,128)S(1)}, u32[]{:S(2)}) copy-start(f32[16,64,256]{2,1,0:T(8,128)S(1)} %get-tuple-element.39) | copy-start | bytes 3145732
  62.0 24.0 %copy-start.3 = (f32[16,64,256]{2,1,0:T(8,128)}, f32[16,64,256]{2,1,0:T(8,128)S(1)}, u32[]{:S(2)}) copy-start(f32[16,64,256]{2,1,0:T(8,128)S(1)} %get-tuple-element.41) | copy-start | bytes 3145732
  62.7 20.2 %collective-permute-start.5 = (f32[2,1024]{1,0:T(2,128)S(1)}, f32[2,1024]{1,0:T(2,128)S(1)}, u32[]{:S(2)}, u32[]{:S(2)}) collective-permute-start(f32[2,1024]{1,0:T(2,128)S(1)} %pad_maximum_fusion.18), channel_id=1, source_target_pairs={{1,0},{2,1},{3,2},{4,3},{5,4},{6,5},{7,6},{9,8},{10,9},{11,10},{12... | collective-permute-start | bytes 24584 | tf_op jit(solution)/shard_map/ppermute | solution.py:20
  80.7 5.2 %collective-permute-start.4 = (f32[2,4096]{1,0:T(2,128)S(1)}, f32[2,4096]{1,0:T(2,128)S(1)}, u32[]{:S(2)}, u32[]{:S(2)}) collective-permute-start(f32[2,4096]{1,0:T(2,128)S(1)} %pad_maximum_fusion.12), channel_id=1, source_target_pairs={{8,0},{16,8},{24,16},{32,24},{40,32},{48,40},{56,48},{64,56},{72,6... | collective-permute-start | bytes 98312 | tf_op jit(solution)/shard_map/ppermute | solution.py:20
  92.4 1.0 copy-start.4
  92.4 1.4 copy-start.8
  92.5 11.3 %copy-start.12 = (f32[16,64,256]{2,1,0:T(8,128)S(1)}, f32[16,64,256]{2,1,0:T(8,128)}, u32[]{:S(2)}) copy-start(f32[16,64,256]{2,1,0:T(8,128)} %get-tuple-element.67) | copy-start | bytes 3145732
  95.3 12.8 %collective-permute-start.6 = (f32[2,1024]{1,0:T(2,128)S(1)}, f32[2,1024]{1,0:T(2,128)S(1)}, u32[]{:S(2)}, u32[]{:S(2)}) collective-permute-start(f32[2,1024]{1,0:T(2,128)S(1)} %pad_maximum_fusion.19), channel_id=1, source_target_pairs={{0,1},{1,2},{2,3},{3,4},{4,5},{5,6},{6,7},{8,9},{9,10},{10,11},{11... | collective-permute-start | bytes 24584 | tf_op jit(solution)/shard_map/ppermute | solution.py:20
  104.9 5.6 %collective-permute-start.7 = (f32[2,4096]{1,0:T(2,128)S(1)}, f32[2,4096]{1,0:T(2,128)S(1)}, u32[]{:S(2)}, u32[]{:S(2)}) collective-permute-start(f32[2,4096]{1,0:T(2,128)S(1)} %pad_maximum_fusion.13), channel_id=1, source_target_pairs={{0,8},{8,16},{16,24},{24,32},{32,40},{40,48},{48,56},{56,64},{64,7... | collective-permute-start | bytes 98312 | tf_op jit(solution)/shard_map/ppermute | solution.py:20
  120.5 20.0 %collective-permute-start.9 = (f32[2,1024]{1,0:T(2,128)S(1)}, f32[2,1024]{1,0:T(2,128)S(1)}, u32[]{:S(2)}, u32[]{:S(2)}) collective-permute-start(f32[2,1024]{1,0:T(2,128)S(1)} %pad_maximum_fusion.20), channel_id=1, source_target_pairs={{1,0},{2,1},{3,2},{4,3},{5,4},{6,5},{7,6},{9,8},{10,9},{11,10},{12... | collective-permute-start | bytes 24584 | tf_op jit(solution)/shard_map/ppermute | solution.py:20
  121.9 10.8 %copy-start.2 = (f32[16,64,256]{2,1,0:T(8,128)S(1)}, f32[16,64,256]{2,1,0:T(8,128)}, u32[]{:S(2)}) copy-start(f32[16,64,256]{2,1,0:T(8,128)} %get-tuple-element.50) | copy-start | bytes 3145732
  138.6 5.2 %collective-permute-start.8 = (f32[2,4096]{1,0:T(2,128)S(1)}, f32[2,4096]{1,0:T(2,128)S(1)}, u32[]{:S(2)}, u32[]{:S(2)}) collective-permute-start(f32[2,4096]{1,0:T(2,128)S(1)} %pad_maximum_fusion.14), channel_id=1, source_target_pairs={{8,0},{16,8},{24,16},{32,24},{40,32},{48,40},{56,48},{64,56},{72,6... | collective-permute-start | bytes 98312 | tf_op jit(solution)/shard_map/ppermute | solution.py:20
  150.3 1.0 copy-start.6
  150.3 1.3 copy-start.10
  153.1 26.2 %collective-permute-start.10 = (f32[2,1024]{1,0:T(2,128)S(1)}, f32[2,1024]{1,0:T(2,128)S(1)}, u32[]{:S(2)}, u32[]{:S(2)}) collective-permute-start(f32[2,1024]{1,0:T(2,128)S(1)} %pad_maximum_fusion.21), channel_id=1, source_target_pairs={{0,1},{1,2},{2,3},{3,4},{4,5},{5,6},{6,7},{8,9},{9,10},{10,11},{11... | collective-permute-start | bytes 24584 | tf_op jit(solution)/shard_map/ppermute | solution.py:20
  164.0 17.6 %collective-permute-start.11 = (f32[2,4096]{1,0:T(2,128)S(1)}, f32[2,4096]{1,0:T(2,128)S(1)}, u32[]{:S(2)}, u32[]{:S(2)}) collective-permute-start(f32[2,4096]{1,0:T(2,128)S(1)} %pad_maximum_fusion.15), channel_id=1, source_target_pairs={{0,8},{8,16},{16,24},{24,32},{32,40},{40,48},{48,56},{56,64},{64,7... | collective-permute-start | bytes 98312 | tf_op jit(solution)/shard_map/ppermute | solution.py:20
  181.6 7.3 %slice-start = ((s8[6291456]{0:T(1024)(128)(4,1)}), s8[4194304]{0:T(1024)(128)(4,1)S(1)}, s32[]{:S(2)}) async-start(s8[6291456]{0:T(1024)(128)(4,1)} %bitcast.190), calls=%async_computation.1 | async-start | bytes 8388608
  181.7 7.3 %slice-start.1 = ((s8[6291456]{0:T(1024)(128)(4,1)}), s8[2097152]{0:T(1024)(128)(4,1)S(1)}, s32[]{:S(2)}) async-start(s8[6291456]{0:T(1024)(128)(4,1)} %bitcast.190), calls=%async_computation.2 | async-start | bytes 4194304
  189.0 7.1 %copy-start.20 = (f32[3,16,64,256]{3,2,1,0:T(8,128)}, f32[3,16,64,256]{3,2,1,0:T(8,128)S(1)}, u32[]{:S(2)}) copy-start(f32[3,16,64,256]{3,2,1,0:T(8,128)S(1)} %pad_maximum_fusion) | copy-start | bytes 9437188
  189.0 7.0 %copy-start.22 = (f32[4,64,256]{2,1,0:T(8,128)S(1)}, f32[4,64,256]{2,1,0:T(8,128)}, u32[]{:S(2)}) copy-start(f32[4,64,256]{2,1,0:T(8,128)} %get-tuple-element.23) | copy-start | bytes 786436
  189.0 7.0 %copy-start.23 = (f32[4,64,256]{2,1,0:T(8,128)S(1)}, f32[4,64,256]{2,1,0:T(8,128)}, u32[]{:S(2)}) copy-start(f32[4,64,256]{2,1,0:T(8,128)} %get-tuple-element.24) | copy-start | bytes 786436
  189.0 7.0 %copy-start.24 = (f32[4,64,256]{2,1,0:T(8,128)S(1)}, f32[4,64,256]{2,1,0:T(8,128)}, u32[]{:S(2)}) copy-start(f32[4,64,256]{2,1,0:T(8,128)} %get-tuple-element.25) | copy-start | bytes 786436
  189.0 7.0 %copy-start.25 = (f32[4,64,256]{2,1,0:T(8,128)S(1)}, f32[4,64,256]{2,1,0:T(8,128)}, u32[]{:S(2)}) copy-start(f32[4,64,256]{2,1,0:T(8,128)} %get-tuple-element.18) | copy-start | bytes 786436
  189.0 7.0 %copy-start.26 = (f32[4,64,256]{2,1,0:T(8,128)S(1)}, f32[4,64,256]{2,1,0:T(8,128)}, u32[]{:S(2)}) copy-start(f32[4,64,256]{2,1,0:T(8,128)} %get-tuple-element.19) | copy-start | bytes 786436
  189.0 7.0 %copy-start.27 = (f32[4,64,256]{2,1,0:T(8,128)S(1)}, f32[4,64,256]{2,1,0:T(8,128)}, u32[]{:S(2)}) copy-start(f32[4,64,256]{2,1,0:T(8,128)} %get-tuple-element.20) | copy-start | bytes 786436
  189.1 7.0 %copy-start.28 = (f32[4,64,256]{2,1,0:T(8,128)S(1)}, f32[4,64,256]{2,1,0:T(8,128)}, u32[]{:S(2)}) copy-start(f32[4,64,256]{2,1,0:T(8,128)} %get-tuple-element.21) | copy-start | bytes 786436
  189.1 7.0 %copy-start.29 = (f32[4,64,256]{2,1,0:T(8,128)S(1)}, f32[4,64,256]{2,1,0:T(8,128)}, u32[]{:S(2)}) copy-start(f32[4,64,256]{2,1,0:T(8,128)} %convert_element_type.89) | copy-start | bytes 786436
  196.4 18.7 %copy-start.15 = (f32[4,4,64,256]{3,2,1,0:T(8,128)}, f32[4,4,64,256]{3,2,1,0:T(8,128)S(1)}, u32[]{:S(2)}) copy-start(f32[4,4,64,256]{3,2,1,0:T(8,128)S(1)} %fusion.111) | copy-start | bytes 3145732
  196.4 4.8 %collective-permute-start.12 = (f32[4,4,3,256]{3,2,1,0:T(4,128)S(1)}, f32[4,4,3,256]{3,2,1,0:T(4,128)S(1)}, u32[]{:S(2)}, u32[]{:S(2)}) collective-permute-start(f32[4,4,3,256]{3,2,1,0:T(4,128)S(1)} %get-tuple-element.60), channel_id=1, source_target_pairs={{0,8},{8,16},{16,24},{24,32},{32,40},{40,48},{48,56},{56,64},{64,7... | collective-permute-start | bytes 147464 | tf_op jit(solution)/shard_map/ppermute | solution.py:28
  199.3 5.6 %collective-permute-start.13 = (f32[4,4,3,256]{3,2,1,0:T(4,128)S(1)}, f32[4,4,3,256]{3,2,1,0:T(4,128)S(1)}, u32[]{:S(2)}, u32[]{:S(2)}) collective-permute-start(f32[4,4,3,256]{3,2,1,0:T(4,128)S(1)} %get-tuple-element.61), channel_id=1, source_target_pairs={{8,0},{16,8},{24,16},{32,24},{40,32},{48,40},{56,48},{64,56},{72,6... | collective-permute-start | bytes 147464 | tf_op jit(solution)/shard_map/ppermute | solution.py:31
  205.8 8.9 %collective-permute-start.15 = (f32[4,4,70,3]{2,1,3,0:T(4,128)S(1)}, f32[4,4,70,3]{2,1,3,0:T(4,128)S(1)}, u32[]{:S(2)}, u32[]{:S(2)}) collective-permute-start(f32[4,4,70,3]{2,1,3,0:T(4,128)S(1)} %copy.58), channel_id=1, source_target_pairs={{1,0},{2,1},{3,2},{4,3},{5,4},{6,5},{7,6},{9,8},{10,9},{11,10},{12... | collective-permute-start | bytes 40328 | tf_op jit(solution)/shard_map/ppermute | solution.py:31
  207.1 7.3 %collective-permute-start.14 = (f32[4,4,70,3]{2,1,3,0:T(4,128)S(1)}, f32[4,4,70,3]{2,1,3,0:T(4,128)S(1)}, u32[]{:S(2)}, u32[]{:S(2)}) collective-permute-start(f32[4,4,70,3]{2,1,3,0:T(4,128)S(1)} %copy.56), channel_id=1, source_target_pairs={{0,1},{1,2},{2,3},{3,4},{4,5},{5,6},{6,7},{8,9},{9,10},{10,11},{11... | collective-permute-start | bytes 40328 | tf_op jit(solution)/shard_map/ppermute | solution.py:28
  215.8 13.1 %copy-start.31 = (s32[1024,1]{0,1:T(1,128)S(1)}, s32[1024,1]{0,1:T(1,128)}, u32[]{:S(2)}) copy-start(s32[1024,1]{0,1:T(1,128)} %param.13) | copy-start | bytes 12292
  215.9 15.5 %copy-start.7 = (f32[16,64,256]{2,1,0:T(8,128)S(1)}, f32[16,64,256]{2,1,0:T(8,128)}, u32[]{:S(2)}) copy-start(f32[16,64,256]{2,1,0:T(8,128)} %copy-done.6) | copy-start | bytes 3145732
  215.9 15.5 %copy-start.11 = (f32[16,64,256]{2,1,0:T(8,128)S(1)}, f32[16,64,256]{2,1,0:T(8,128)}, u32[]{:S(2)}) copy-start(f32[16,64,256]{2,1,0:T(8,128)} %copy-done.10) | copy-start | bytes 3145732
  215.9 15.5 %copy-start.14 = (f32[16,64,256]{2,1,0:T(8,128)S(1)}, f32[16,64,256]{2,1,0:T(8,128)}, u32[]{:S(2)}) copy-start(f32[16,64,256]{2,1,0:T(8,128)} %get-tuple-element.64) | copy-start | bytes 3145732
Sparse Core Ops, SparseCore 0:
  228.5 104.1 all-gather.1
where the time goes:
time: 362 us; the launch traced here: 358 us
  waiting for transfers between devices  105 us (29%)
  other arithmetic  88.1 us (24%)
  local copies, waits for them, and re-layouts  68.6 us (19%)
  starting transfers between devices  64.5 us (18%)
  matrix products  16.8 us (5%)
  between operations  15.2 us (4%)
    all_gather x1, waiting for transfers between devices, body(): lax.all_gather(filtered, 'gx', axis=2, tiled=True)  99.4 us
    ppermute x12, starting transfers between devices, shifted(): lax.ppermute(value, axis, [(source, source + steps) for source in range(l...  51.9 us
    reduce_sum x3, other arithmetic, spectral_term(): terms.append(jnp.sum(weight * design, axis=0))  26.4 us
    sub x3, other arithmetic, advance(): magnetic[0] - COURANT * (plus_y(elec_z, upper_y[1]) - plus_z(elec_y))  19.4 us
    dot_general x1, matrix products, body(): jnp.einsum('sr,fprc->fpsc', picker, lax.all_gather(filtered, 'gx', axis=2...  16.8 us
    add x2, other arithmetic, advance(): elec_x + COURANT * inverse[0] * (minus_y(magn_z, lower_y[1]) - minus_z(ma...  15.8 us
    div x1, other arithmetic, body(): filtered = total / normal  12.5 us
    slice x6, local copies, waits for them, and re-layouts, minus_z(): field[:-1]  11.1 us
  transfers between devices with their start and end apart: 17, of which 5 were waited for; matrix products, arithmetic and copies ran while one was open for 21% of the time, Pallas kernels for 0%

commit v1 on v0

v1 whole, which is shorter than its diff:
```python
import functools
import math

import jax
import jax.numpy as jnp
from jax import lax
from jax.experimental import pallas as pl
from jax.experimental.pallas import tpu as pltpu
from jax.sharding import PartitionSpec as P

MESH = pl.DeviceIdType.MESH
F32 = jnp.float32

NZ = 16
ROWS = 64
COLS = 256
TOP = 8
LEFT = 128
XROWS = 80
XCOLS = 384
DP = 4
FIRST = 6
FREQ = 4
RADIUS = 3
CAP = 8
COURANT = 0.5

PIECES = (
    (0, 0, 3, 0), (0, 1, 3, 3), (2, 0, 2, 6),
    (0, 2, 3, 8), (1, 0, 3, 11), (2, 1, 2, 14),
    (1, 1, 3, 16), (1, 2, 3, 19), (2, 2, 2, 22),
)
INNER = tuple(range(3, 13))
OUTER = (0, 1, 2, 13, 14, 15)


def weight(shift_x, shift_y):
    return RADIUS + 1.0 - math.sqrt(shift_x * shift_x + shift_y * shift_y)


def roll(value, shift, axis):
    shift = shift % value.shape[axis]
    return value if shift == 0 else pltpu.roll(value, shift, axis)


def tile_rows(tile):
    return pl.ds(pl.multiple_of(tile * 8, 8), 8)


def kernel(
    n_x, n_y,
    elec_in, magn_in, perm_in, spec_in, freq_in, mask_in, owner_in,
    elec_out, magn_out, owned_out,
    elec, magn, perm, spec, mask, coef, trig, early, masked, inverse_norm, picker,
    fold, plane_out, packed,
    ysend_i, yrecv_i, xsend_i, xrecv_i,
    ysend_o, yrecv_o, xsend_o, xrecv_o,
    ysend_m, yrecv_m, xsend_m, xrecv_m,
    load_sem, save_sem, own_sem, send_sem, recv_sem, route_send, route_recv,
):
    gx = lax.axis_index("gx")
    gy = lax.axis_index("gy")
    x_up, x_down = lax.rem(gx + 1, n_x), lax.rem(gx + n_x - 1, n_x)
    y_up, y_down = lax.rem(gy + 1, n_y), lax.rem(gy + n_y - 1, n_y)

    own_r, own_c = pl.ds(TOP, ROWS), pl.ds(LEFT, COLS)

    def load(source, target, first, count, shift, sem):
        return pltpu.make_async_copy(
            source.at[:, pl.ds(first, count)],
            target.at[:, pl.ds(first + shift, count), own_r, own_c],
            load_sem.at[sem],
        )

    loads_i = [
        load(elec_in, elec, 3, 10, 0, 0),
        load(magn_in, magn, 3, 10, 1, 1),
        load(perm_in, perm, 3, 10, 0, 2),
    ]
    loads_o = [
        load(elec_in, elec, 0, 3, 0, 3), load(elec_in, elec, 13, 3, 0, 4),
        load(magn_in, magn, 0, 3, 1, 5), load(magn_in, magn, 13, 3, 1, 6),
        load(perm_in, perm, 0, 3, 0, 7), load(perm_in, perm, 13, 3, 0, 8),
    ]
    loads_s = [
        pltpu.make_async_copy(spec_in, spec, load_sem.at[9]),
        pltpu.make_async_copy(mask_in, mask, load_sem.at[10]),
    ]
    for copy in loads_i:
        copy.start()
    for copy in loads_o:
        copy.start()
    for copy in loads_s:
        copy.start()

    barrier = pltpu.get_barrier_semaphore()
    greeted = [(lax.rem(gx + k, n_x), gy) for k in range(1, n_x)]
    greeted += [(x, y) for x in (x_down, gx, x_up) for y in (y_down, y_up)]
    for peer in greeted:
        pl.semaphore_signal(barrier, inc=1, device_id=peer, device_id_type=MESH)

    lane = lax.broadcasted_iota(jnp.int32, (8, 128), 1)
    lanes = lax.broadcasted_iota(jnp.int32, (8, XCOLS), 1)
    sub3 = lax.broadcasted_iota(jnp.int32, (8, XCOLS), 0)
    sub = lax.broadcasted_iota(jnp.int32, (8, COLS), 0)
    has_down = jnp.where(gx > 0, 1.0, 0.0).astype(F32)
    has_up = jnp.where(gx < n_x - 1, 1.0, 0.0).astype(F32)
    has_left = jnp.where(gy > 0, 1.0, 0.0).astype(F32)
    has_right = jnp.where(gy < n_y - 1, 1.0, 0.0).astype(F32)

    for c in range(3):
        elec[c, NZ] = jnp.zeros((XROWS, XCOLS), F32)
        magn[c, 0] = jnp.zeros((XROWS, XCOLS), F32)

    half = jnp.where((lanes >= 64) & (lanes < 128), COURANT * has_left, COURANT)
    for t in range(10):
        coef[8 * t:8 * t + 8, :] = half * has_down if t == 0 else half

    for f in range(FREQ):
        for s in range(3):
            angle = jnp.full((8, 128), freq_in[f] * (s + 1.0), F32)
            trig[f, s, 0] = jnp.cos(angle)
            trig[f, s, 1] = jnp.sin(angle)

    col = gy * COLS + lax.broadcasted_iota(jnp.int32, (8, COLS), 1)
    inside = [
        ((col + b >= 0) & (col + b < n_y * COLS)).astype(F32) for b in range(-RADIUS, RADIUS + 1)
    ]
    sums = []
    for a in range(RADIUS + 1):
        total = jnp.zeros((8, COLS), F32)
        for b in range(-RADIUS, RADIUS + 1):
            if weight(a, b) > 0.0:
                total = total + weight(a, b) * inside[b + RADIUS]
        sums.append(total)

    def norm_tile(t, carry):
        row = gx * ROWS + t * 8 + sub
        total = jnp.zeros((8, COLS), F32)
        for a in range(-RADIUS, RADIUS + 1):
            within = ((row + a >= 0) & (row + a < n_x * ROWS)).astype(F32)
            total = total + within * sums[abs(a)]
        inverse_norm[tile_rows(t), :] = 1.0 / total
        return carry

    lax.fori_loop(0, ROWS // 8, norm_tile, 0)

    owners = owner_in[pl.ds(gx // 2, 1), :].astype(F32)
    lane1 = lax.broadcasted_iota(jnp.int32, (1, 128), 1)
    other = pltpu.roll(owners, 64, 1)
    low_half = lane1 < 64
    even = (lax.rem(gx, 2) == 0)
    keep = jnp.where(even, owners, other)
    swap = jnp.where(even, other, owners)
    owners = jnp.where(low_half, keep, pltpu.roll(keep, 64, 1))
    del swap
    rows_i = lax.broadcasted_iota(jnp.int32, (ROWS, 128), 0)
    lanes_j = lax.broadcasted_iota(jnp.int32, (ROWS, 128), 1)
    owners_b = jnp.broadcast_to(owners, (ROWS, 128))
    column = jnp.sum(jnp.where(rows_i == lanes_j, owners_b, 0.0), axis=1, keepdims=True)
    earlier = rows_i < jnp.where(lanes_j < 64, lanes_j, lanes_j - 64)
    same = jnp.where((column == owners_b) & earlier, 1.0, 0.0)
    slot = owners * CAP + jnp.sum(same, axis=0, keepdims=True)
    slots = jnp.concatenate([slot, slot], axis=1)
    wanted = lax.broadcasted_iota(jnp.int32, (n_x * CAP, 256), 0).astype(F32)
    used = lax.broadcasted_iota(jnp.int32, (n_x * CAP, 256), 1) < 3 * ROWS
    picker[...] = jnp.where((wanted == slots) & used, 1.0, 0.0).astype(jnp.bfloat16)

    fields = (elec, magn, perm)

    def plane_of(kind, p):
        return p + 1 if kind == 1 else p

    def pack(planes, at, ysend, xsend):
        def pack_y(t, carry):
            rows = pl.ds(pl.multiple_of(TOP + t * 8, 8), 8)
            for side in range(2):
                for group in range(2):
                    parts = jnp.zeros((8, 128), F32)
                    for i, p in enumerate(planes[5 * group:5 * group + 5]):
                        for kind, c, width, place in PIECES:
                            target = 24 * i + place
                            ref = fields[kind].at[c, plane_of(kind, p)]
                            if side == 0:
                                piece = ref[rows, pl.ds(2 * 128, 128)]
                                piece = roll(piece, target - (128 - width), 1)
                            else:
                                piece = ref[rows, pl.ds(128, 128)]
                                piece = roll(piece, target, 1)
                            parts = jnp.where(lane < target, parts, piece)
                    ysend[side, tile_rows(t), group * 128:group * 128 + 128] = parts
            return carry

        lax.fori_loop(0, ROWS // 8, pack_y, 0)

        def pack_x(q, carry):
            p = at(q)
            for side in range(2):
                start = TOP + ROWS - 8 if side == 0 else TOP
                for group in range(3):
                    parts = None
                    for kind, c, width, place in PIECES[3 * group:3 * group + 3]:
                        target = place - 8 * group
                        piece = fields[kind][c, plane_of(kind, p), start:start + 8, LEFT:XCOLS]
                        piece = roll(piece, target - (8 - width) if side == 0 else target, 0)
                        parts = piece if parts is None else jnp.where(sub < target, parts, piece)
                    xsend[side, q, 8 * group:8 * group + 8, :] = parts
            return carry

        lax.fori_loop(0, len(planes), pack_x, 0)

    def exchange(stage, ysend, yrecv, xsend, xrecv):
        plan = [
            (xsend.at[0], xrecv.at[0], (x_up, gy)),
            (xsend.at[1], xrecv.at[1], (x_down, gy)),
        ]
        for side, y in ((0, y_up), (1, y_down)):
            plan += [
                (ysend.at[side], yrecv.at[side, pl.ds(TOP, ROWS)], (gx, y)),
                (ysend.at[side, pl.ds(ROWS - 8, 8)], yrecv.at[side, pl.ds(0, 8)], (x_up, y)),
                (ysend.at[side, pl.ds(0, 8)], yrecv.at[side, pl.ds(TOP + ROWS, 8)], (x_down, y)),
            ]
        return [
            pltpu.make_async_remote_copy(
                src_ref=source, dst_ref=target,
                send_sem=send_sem.at[stage, i], recv_sem=recv_sem.at[stage, i],
                device_id=peer, device_id_type=MESH,
            )
            for i, (source, target, peer) in enumerate(plan)
        ]

    def unpack(planes, at, yrecv, xrecv):
        def unpack_y(t, carry):
            rows = tile_rows(t)
            there = jnp.where(t == 0, has_down, jnp.where(t == 9, has_up, 1.0))
            for group in range(2):
                if not planes[5 * group:5 * group + 5]:
                    continue
                cols = pl.ds(group * 128, 128)
                low = yrecv[0, rows, cols] * (there * has_left)
                high = yrecv[1, rows, cols] * (there * has_right)
                for i, p in enumerate(planes[5 * group:5 * group + 5]):
                    for kind, c, width, place in PIECES:
                        target = 24 * i + place
                        piece = jnp.where(
                            lane < 64, roll(high, -target, 1), roll(low, 128 - width - target, 1)
                        )
                        fields[kind].at[c, plane_of(kind, p)][rows, pl.ds(0, 128)] = piece
            return carry

        lax.fori_loop(0, XROWS // 8, unpack_y, 0)

        def unpack_x(q, carry):
            p = at(q)
            for side in range(2):
                start = 0 if side == 0 else TOP + ROWS
                for group in range(3):
                    parts = xrecv[side, q, 8 * group:8 * group + 8, :]
                    parts = parts * (has_down if side == 0 else has_up)
                    for kind, c, width, place in PIECES[3 * group:3 * group + 3]:
                        target = place - 8 * group
                        shift = 8 - width - target if side == 0 else -target
                        fields[kind][c, plane_of(kind, p), start:start + 8, LEFT:XCOLS] = roll(
                            parts, shift, 0
                        )
            return carry

        lax.fori_loop(0, len(planes), unpack_x, 0)

    def ahead_x(ref, c, p, t, value):
        if t == 9:
            return pltpu.roll(value, 7, 0)
        return pltpu.roll(jnp.where(sub3 == 0, ref[c, p, 8 * t + 8:8 * t + 16, :], value), 7, 0)

    def behind_x(ref, c, p, t, value):
        if t == 0:
            return pltpu.roll(value, 1, 0)
        return pltpu.roll(jnp.where(sub3 == 7, ref[c, p, 8 * t - 8:8 * t, :], value), 1, 0)

    def magnetic(start, stop):
        def one(p, carry):
            for t in range(10):
                rows = slice(8 * t, 8 * t + 8)
                ex, ey, ez = (elec[c, p, rows, :] for c in range(3))
                factor = coef[rows, :]
                ez_y = pltpu.roll(ez, XCOLS - 1, 1)
                ex_y = pltpu.roll(ex, XCOLS - 1, 1)
                ez_x = ahead_x(elec, 2, p, t, ez)
                ey_x = ahead_x(elec, 1, p, t, ey)
                q = p + 1
                magn[0, q, rows, :] -= factor * ((ez_y - ez) - (elec[1, q, rows, :] - ey))
                magn[1, q, rows, :] -= factor * ((elec[0, q, rows, :] - ex) - (ez_x - ez))
                magn[2, q, rows, :] -= factor * ((ey_x - ey) - (ex_y - ex))
            return carry

        lax.fori_loop(start, stop, one, 0)

    def electric(start, stop):
        def one(p, carry):
            for t in range(10):
                rows = slice(8 * t, 8 * t + 8)
                q = p + 1
                hx, hy, hz = (magn[c, q, rows, :] for c in range(3))
                hz_y = pltpu.roll(hz, 1, 1)
                hx_y = pltpu.roll(hx, 1, 1)
                hz_x = behind_x(magn, 2, q, t, hz)
                hy_x = behind_x(magn, 1, q, t, hy)
                elec[0, p, rows, :] += (COURANT * perm[0, p, rows, :]) * (
                    (hz - hz_y) - (hy - magn[1, p, rows, :])
                )
                elec[1, p, rows, :] += (COURANT * perm[1, p, rows, :]) * (
                    (hx - magn[0, p, rows, :]) - (hz - hz_x)
                )
                elec[2, p, rows, :] += (COURANT * perm[2, p, rows, :]) * (
                    (hy - hy_x) - (hx - hx_y)
                )
            return carry

        lax.fori_loop(start, stop, one, 0)

    for copy in loads_i:
        copy.wait()
    pack(INNER, lambda q: q + 3, ysend_i, xsend_i)
    pl.semaphore_wait(barrier, len(greeted))
    copies_i = exchange(0, ysend_i, yrecv_i, xsend_i, xrecv_i)
    for copy in copies_i:
        copy.start()
    for copy in loads_o:
        copy.wait()
    outer_at = lambda q: q + 10 * (q // 3)
    pack(OUTER, outer_at, ysend_o, xsend_o)
    for copy in copies_i:
        copy.wait()
    copies_o = exchange(1, ysend_o, yrecv_o, xsend_o, xrecv_o)
    for copy in copies_o:
        copy.start()
    unpack(INNER, lambda q: q + 3, yrecv_i, xrecv_i)

    for s in range(3):
        magnetic(3 + s, 12 - s)
        electric(4 + s, 12 - s)
        if s < 2:
            def keep_plane(p, carry, s=s):
                for c in range(3):
                    early[s, c, p] = elec[c, FIRST + p, TOP:TOP + ROWS, LEFT:XCOLS]
                return carry

            lax.fori_loop(0, DP, keep_plane, 0)

    for copy in loads_s:
        copy.wait()

    def gradient(k, carry):
        p, t = k // 8, lax.rem(k, 8)
        rows = tile_rows(t)
        ext = pl.ds(pl.multiple_of(TOP + t * 8, 8), 8)
        for h in range(2):
            cols = slice(128 * h, 128 * h + 128)
            far = slice(LEFT + 128 * h, LEFT + 128 * h + 128)
            fields_e = [
                [early[0, c, p, rows, cols], early[1, c, p, rows, cols], elec[c, FIRST + p, ext, far]]
                for c in range(3)
            ]
            keep = mask[p, rows, cols].astype(F32)
            for f in range(FREQ):
                total = jnp.zeros((8, 128), F32)
                for part in range(2):
                    w1, w2, w3 = (trig[f, s, part] for s in range(3))
                    for c in range(3):
                        e1, e2, e3 = fields_e[c]
                        total = total + spec[f, part, c, p, rows, cols] * (
                            w1 * e1 + w2 * e2 + w3 * e3
                        )
                masked[f * DP + p, ext, far] = total * keep
        return carry

    lax.fori_loop(0, DP * 8, gradient, 0)

    def edges_y(t, carry):
        ext = pl.ds(pl.multiple_of(TOP + t * 8, 8), 8)
        for side in range(2):
            parts = jnp.zeros((8, 128), F32)
            for m in range(FREQ * DP):
                if side == 0:
                    piece = roll(masked[m, ext, 256:384], 3 * m + 3, 1)
                else:
                    piece = roll(masked[m, ext, 128:256], 3 * m, 1)
                parts = jnp.where(lane < 3 * m, parts, piece)
            ysend_m[side, tile_rows(t), :] = parts
        return carry

    lax.fori_loop(0, ROWS // 8, edges_y, 0)

    def edges_x(j, carry):
        for side in range(2):
            start = TOP + ROWS - 8 if side == 0 else TOP
            first = masked[2 * j, start:start + 8, LEFT:XCOLS]
            second = pltpu.roll(masked[2 * j + 1, start:start + 8, LEFT:XCOLS], 3, 0)
            if side == 0:
                parts = jnp.where(sub < 3, second, first)
            else:
                parts = jnp.where(sub < 3, first, second)
            xsend_m[side, tile_rows(j), :] = parts
        return carry

    lax.fori_loop(0, FREQ * DP // 2, edges_x, 0)

    copies_m = exchange(2, ysend_m, yrecv_m, xsend_m, xrecv_m)
    for copy in copies_m:
        copy.start()
    for copy in copies_m:
        copy.wait()

    def put_y(t, carry):
        rows = tile_rows(t)
        there = jnp.where(t == 0, has_down, jnp.where(t == 9, has_up, 1.0))
        low = yrecv_m[0, rows, :] * (there * has_left)
        high = yrecv_m[1, rows, :] * (there * has_right)
        for m in range(FREQ * DP):
            masked[m, rows, 0:128] = jnp.where(
                lane < 64, roll(high, -3 * m, 1), roll(low, 125 - 3 * m, 1)
            )
        return carry

    lax.fori_loop(0, XROWS // 8, put_y, 0)

    def put_x(j, carry):
        for side in range(2):
            start = 0 if side == 0 else TOP + ROWS
            parts = xrecv_m[side, tile_rows(j), :] * (has_down if side == 0 else has_up)
            masked[2 * j, start:start + 8, LEFT:XCOLS] = parts
            masked[2 * j + 1, start:start + 8, LEFT:XCOLS] = pltpu.roll(parts, 5, 0)
        return carry

    lax.fori_loop(0, FREQ * DP // 2, put_x, 0)

    routes = []
    for f in range(FREQ):
        def filter_plane(p, carry, f=f):
            m = f * DP + p
            for t in range(10):
                value = masked[m, 8 * t:8 * t + 8, :]
                center = value[:, LEFT:XCOLS]
                pairs = [
                    (pltpu.roll(value, b, 1) + pltpu.roll(value, XCOLS - b, 1))[:, LEFT:XCOLS]
                    for b in range(1, RADIUS + 1)
                ]
                for a in range(RADIUS + 1):
                    if a == 0 and t in (0, 9):
                        continue
                    total = weight(a, 0) * center
                    for b in range(1, RADIUS + 1):
                        if weight(a, b) > 0.0:
                            total = total + weight(a, b) * pairs[b - 1]
                    fold[a, 8 * t:8 * t + 8, :] = total
            for t in range(1, 9):
                total = fold[0, 8 * t:8 * t + 8, :]
                for a in range(1, RADIUS + 1):
                    here = fold[a, 8 * t:8 * t + 8, :]
                    after = fold[a, 8 * t + 8:8 * t + 16, :]
                    before = fold[a, 8 * t - 8:8 * t, :]
                    total = total + pltpu.roll(jnp.where(sub < a, after, here), 8 - a, 0)
                    total = total + pltpu.roll(jnp.where(sub >= 8 - a, before, here), a, 0)
                plane_out[8 * t - 8:8 * t, :] = total * inverse_norm[8 * t - 8:8 * t, :]
            value = plane_out[...]
            high = value.astype(jnp.bfloat16)
            rest = value - high.astype(F32)
            middle = rest.astype(jnp.bfloat16)
            low = (rest - middle.astype(F32)).astype(jnp.bfloat16)
            stacked = jnp.concatenate([high, middle, low, jnp.zeros_like(low)], axis=0)
            packed[f, p] = jnp.dot(picker[...], stacked, preferred_element_type=F32)
            return carry

        lax.fori_loop(0, DP, filter_plane, 0)
        mine = pl.ds(pl.multiple_of(gx * CAP, CAP), CAP)
        for k in list(range(n_x // 2, n_x)) + list(range(1, n_x // 2)):
            owner = gx ^ k
            theirs = pl.ds(pl.multiple_of(owner * CAP, CAP), CAP)
            copy = pltpu.make_async_remote_copy(
                src_ref=packed.at[f, :, theirs], dst_ref=owned_out.at[f, :, mine],
                send_sem=route_send.at[f, k], recv_sem=route_recv.at[f, k],
                device_id=(owner, gy), device_id_type=MESH,
            )
            copy.start()
            routes.append(copy)
        copy = pltpu.make_async_copy(packed.at[f, :, mine], owned_out.at[f, :, mine], own_sem.at[f])
        copy.start()
        routes.append(copy)

    for copy in copies_o:
        copy.wait()
    unpack(OUTER, outer_at, yrecv_o, xrecv_o)
    for s in range(3):
        magnetic(12 - s, NZ)
        magnetic(0, 3 + s)
        electric(12 - s, NZ)
        electric(0, 4 + s)
    saves = [
        pltpu.make_async_copy(elec.at[:, pl.ds(0, NZ), own_r, own_c], elec_out, save_sem.at[0]),
        pltpu.make_async_copy(magn.at[:, pl.ds(1, NZ), own_r, own_c], magn_out, save_sem.at[1]),
    ]
    for copy in saves:
        copy.start()
    for copy in routes:
        copy.wait()
    for copy in saves:
        copy.wait()


def body(n_x, n_y, elec, magn, perm, spec, freq, mask, owner):
    any_space = pl.BlockSpec(memory_space=pl.ANY)
    vmem = pl.BlockSpec(memory_space=pltpu.VMEM)
    smem = pl.BlockSpec(memory_space=pltpu.SMEM)
    buf = pltpu.VMEM
    sem = pltpu.SemaphoreType.DMA
    return pl.pallas_call(
        functools.partial(kernel, n_x, n_y),
        out_shape=(
            jax.ShapeDtypeStruct((3, NZ, ROWS, COLS), F32),
            jax.ShapeDtypeStruct((3, NZ, ROWS, COLS), F32),
            jax.ShapeDtypeStruct((FREQ, DP, n_x * CAP, COLS), F32),
        ),
        in_specs=[any_space] * 4 + [smem, any_space, vmem],
        out_specs=(OUT_SPACE, OUT_SPACE, OUT_SPACE),
        scratch_shapes=[
            buf((3, NZ + 1, XROWS, XCOLS), F32),
            buf((3, NZ + 1, XROWS, XCOLS), F32),
            buf((3, NZ, XROWS, XCOLS), F32),
            buf((FREQ, 2, 3, DP, ROWS, COLS), F32),
            buf((DP, ROWS, COLS), jnp.int32),
            buf((XROWS, XCOLS), F32),
            buf((FREQ, 3, 2, 8, 128), F32),
            buf((2, 3, DP, ROWS, COLS), F32),
            buf((FREQ * DP, XROWS, XCOLS), F32),
            buf((ROWS, COLS), F32),
            buf((n_x * CAP, 256), jnp.bfloat16),
            buf((RADIUS + 1, XROWS, COLS), F32),
            buf((ROWS, COLS), F32),
            buf((FREQ, DP, n_x * CAP, COLS), F32),
            buf((2, ROWS, 256), F32), buf((2, XROWS, 256), F32),
            buf((2, len(INNER), 24, COLS), F32), buf((2, len(INNER), 24, COLS), F32),
            buf((2, ROWS, 256), F32), buf((2, XROWS, 256), F32),
            buf((2, len(OUTER), 24, COLS), F32), buf((2, len(OUTER), 24, COLS), F32),
            buf((2, ROWS, 128), F32), buf((2, XROWS, 128), F32),
            buf((2, ROWS, COLS), F32), buf((2, ROWS, COLS), F32),
            sem((11,)), sem((2,)), sem((FREQ,)), sem((3, 8)), sem((3, 8)),
            sem((FREQ, n_x)), sem((FREQ, n_x)),
        ],
        compiler_params=pltpu.CompilerParams(
            collective_id=0, has_side_effects=True, vmem_limit_bytes=52 << 20
        ),
        name="adjoint",
    )(elec, magn, perm, spec, freq, mask, owner.reshape(8, 128))


OUT_SPACE = pl.BlockSpec(memory_space=pl.ANY)


def solution(mesh):
    placed = (
        P(None, None, "gx", "gy"),
        P(None, None, "gx", "gy"),
        P(None, None, "gx", "gy"),
        P(None, None, None, None, "gx", "gy"),
        P(),
        P(None, "gx", "gy"),
        P(),
    )
    return jax.shard_map(
        functools.partial(body, mesh.shape["gx"], mesh.shape["gy"]),
        mesh=mesh,
        in_specs=placed,
        out_specs=(P(None, None, "gx", "gy"), P(None, None, "gx", "gy"), P(None, None, "gx", "gy")),
        check_vma=False,
    )
```

time: 362 us -> 77.8 us (0.21)
  waiting for transfers between devices: 105 us -> 0 us
  other arithmetic: 88.1 us -> 0 us
  Pallas kernels: 0 us -> 66.5 us
  starting transfers between devices: 64.5 us -> 0 us
  local copies, waits for them, and re-layouts: 68.6 us -> 10.4 us
  matrix products: 16.8 us -> 0 us
  between operations: 15.2 us -> 0.66 us
    all_gather x1 -> x0, waiting for transfers between devices: 99.4 us -> none  [body(): lax.all_gather(filtered, 'gx', axis=2, tiled=True)]
    pallas_call x0 -> x1, Pallas kernels: none -> 66.5 us  [body(): pl.pallas_call(functools.partial(kernel, n_x, n_y), out_shape=(jax.ShapeD...]
    ppermute x16 -> x0, starting transfers between devices: 64.4 us -> none  [the longest x12 51.9 us: shifted(): lax.ppermute(value, axis, [(source, source + steps) for source in range(l...]
    slice x65 -> x0, local copies, waits for them, and re-layouts: 43.4 us -> none  [the longest x6 11.1 us: minus_z(): field[:-1]]
    reduce_sum x3 -> x0, other arithmetic: 26.4 us -> none  [spectral_term(): terms.append(jnp.sum(weight * design, axis=0))]
    sub x3 -> x0, other arithmetic: 19.4 us -> none  [advance(): magnetic[0] - COURANT * (plus_y(elec_z, upper_y[1]) - plus_z(elec_y))]
    dot_general x1 -> x0, matrix products: 16.8 us -> none  [body(): jnp.einsum('sr,fprc->fpsc', picker, lax.all_gather(filtered, 'gx', axis=2...]
    add x3 -> x0, other arithmetic: 16.2 us -> none  [the longest x2 15.8 us: advance(): elec_x + COURANT * inverse[0] * (minus_y(magn_z, lower_y[1]) - minus_z(ma...]
  transfers between devices with their start and end apart: 17 -> 0, of which waited for: 5 -> 0; matrix products, arithmetic and copies ran while one was open for 21% -> 0% of each run, Pallas kernels for 0% -> 0%
where the time goes in v1:
time: 77.8 us; the launch traced here: 77.5 us
  Pallas kernels  66.5 us (85%)
  local copies, waits for them, and re-layouts  10.4 us (13%)
    pallas_call x1, Pallas kernels, body(): pl.pallas_call(functools.partial(kernel, n_x, n_y), out_shape=(jax.ShapeD...  66.5 us
    unnamed x13, local copies, waits for them, and re-layouts  10.4 us

profile of v1, /device:TPU:1, one launch (start us, length us, event | category | flops | bytes accessed | tf_op | source)
XLA Modules:
  0.0 77.5 jit_solution(3336665597339117800)
XLA Ops:
  0.6 0.0 copy-start
  0.6 0.9 %copy-done = s32[4,64,256]{2,1,0:T(8,128)S(1)} copy-done((s32[4,64,256]{2,1,0:T(8,128)S(1)}, s32[4,64,256]{2,1,0:T(8,128)}, u32[]{:S(2)}) %copy-start) | copy-done | bytes 262168
  1.6 0.0 copy-start.1
  1.6 0.7 copy-done.1
  2.3 0.0 copy-start.2
  2.3 0.7 copy-done.2
  2.9 66.5 %adjoint.1 = (f32[3,16,64,256]{3,2,1,0:T(8,128)}, f32[3,16,64,256]{3,2,1,0:T(8,128)}, f32[4,4,128,256]{3,2,1,0:T(8,128)}) custom-call(f32[3,16,64,256]{3,2,1,0:T(8,128)} %elec_in.1, f32[3,16,64,256]{3,2,1,0:T(8,128)} %magn_in.1, f32[3,16,64,256]{3,2,1,0:T(8,128)} %perm_in.1, f32[4,2,3,4,64,256]{5,4,3,2,1,0:T(8,128)} %spec_in.1, f32[4]{0:T(128)S(1)} %copy-done.2, ...), custom_call_target="tpu_custom_call" | custom-call | tf_op jit(solution)/shard_map/adjoint/pallas_call | solution.py:516
  69.4 0.0 copy-start.3
  69.4 4.1 %copy.13 = f32[3,16,64,256]{3,2,1,0:T(8,128)} copy(f32[3,16,64,256]{3,2,1,0:T(8,128)} %get-tuple-element.6) | data formatting | bytes 6291456
  73.5 0.0 copy-done.3
  73.5 0.0 copy-start.4
  73.5 1.7 %copy.14 = f32[3,16,64,256]{3,2,1,0:T(8,128)} copy(f32[3,16,64,256]{3,2,1,0:T(8,128)S(1)} %copy-done.3) | data formatting | bytes 6291456
  75.2 1.1 %copy-done.4 = f32[4,4,128,256]{3,2,1,0:T(8,128)S(1)} copy-done((f32[4,4,128,256]{3,2,1,0:T(8,128)S(1)}, f32[4,4,128,256]{3,2,1,0:T(8,128)}, u32[]{:S(2)}) %copy-start.4) | copy-done | bytes 2097176
  76.2 1.3 %copy.15 = f32[4,4,128,256]{3,2,1,0:T(8,128)} copy(f32[4,4,128,256]{3,2,1,0:T(8,128)S(1)} %copy-done.4) | data formatting | bytes 4194304
Async XLA Ops:
  0.6 1.0 %copy-start = (s32[4,64,256]{2,1,0:T(8,128)S(1)}, s32[4,64,256]{2,1,0:T(8,128)}, u32[]{:S(2)}) copy-start(s32[4,64,256]{2,1,0:T(8,128)} %mask_in.1) | copy-start | bytes 786436
  1.6 0.7 copy-start.1
  2.3 0.7 copy-start.2
  69.4 4.1 %copy-start.3 = (f32[3,16,64,256]{3,2,1,0:T(8,128)S(1)}, f32[3,16,64,256]{3,2,1,0:T(8,128)}, u32[]{:S(2)}) copy-start(f32[3,16,64,256]{3,2,1,0:T(8,128)} %get-tuple-element.7) | copy-start | bytes 9437188
  73.5 2.7 %copy-start.4 = (f32[4,4,128,256]{3,2,1,0:T(8,128)S(1)}, f32[4,4,128,256]{3,2,1,0:T(8,128)}, u32[]{:S(2)}) copy-start(f32[4,4,128,256]{3,2,1,0:T(8,128)} %get-tuple-element.8) | copy-start | bytes 6291460

commit v2 on v1

--- a/solution.py
+++ b/solution.py
@@ -49,14 +49,14 @@
 
 def kernel(
     n_x, n_y,
-    elec_in, magn_in, perm_in, spec_in, freq_in, mask_in, owner_in,
-    elec_out, magn_out, owned_out,
-    elec, magn, perm, spec, mask, coef, trig, early, masked, inverse_norm, picker,
+    elec_in, magn_in, perm_in, spec_in, freq_hbm, mask_in, owner_hbm,
+    elec, magn, owned_out,
+    perm, spec, freq_in, mask, owner_in, trig, early, masked, inverse_norm, picker,
     fold, plane_out, packed,
     ysend_i, yrecv_i, xsend_i, xrecv_i,
     ysend_o, yrecv_o, xsend_o, xrecv_o,
     ysend_m, yrecv_m, xsend_m, xrecv_m,
-    load_sem, save_sem, own_sem, send_sem, recv_sem, route_send, route_recv,
+    load_sem, own_sem, send_sem, recv_sem, route_send, route_recv,
 ):
     gx = lax.axis_index("gx")
     gy = lax.axis_index("gy")
@@ -86,6 +86,12 @@
         pltpu.make_async_copy(spec_in, spec, load_sem.at[9]),
         pltpu.make_async_copy(mask_in, mask, load_sem.at[10]),
     ]
+    loads_t = [
+        pltpu.make_async_copy(freq_hbm, freq_in, load_sem.at[11]),
+        pltpu.make_async_copy(owner_hbm, owner_in, load_sem.at[12]),
+    ]
+    for copy in loads_t:
+        copy.start()
     for copy in loads_i:
         copy.start()
     for copy in loads_o:
@@ -108,19 +114,204 @@
     has_left = jnp.where(gy > 0, 1.0, 0.0).astype(F32)
     has_right = jnp.where(gy < n_y - 1, 1.0, 0.0).astype(F32)
 
+    fields = (elec, magn, perm)
+
+    half = jnp.where((lanes >= 64) & (lanes < 128), COURANT * has_left, COURANT)
+    corner = half * has_down
+
+    def plane_of(kind, p):
+        return p + 1 if kind == 1 else p
+
+    def pack_rows_y(planes, ysend):
+        def pack_y(t, carry):
+            rows = pl.ds(pl.multiple_of(TOP + t * 8, 8), 8)
+            for side in range(2):
+                for group in range(2):
+                    parts = jnp.zeros((8, 128), F32)
+                    for i, p in enumerate(planes[5 * group:5 * group + 5]):
+                        for kind, c, width, place in PIECES:
+                            target = 24 * i + place
+                            ref = fields[kind].at[c, plane_of(kind, p)]
+                            if side == 0:
+                                piece = ref[rows, pl.ds(2 * 128, 128)]
+                                piece = roll(piece, target - (128 - width), 1)
+                            else:
+                                piece = ref[rows, pl.ds(128, 128)]
+                                piece = roll(piece, target, 1)
+                            parts = jnp.where(lane < target, parts, piece)
+                    ysend[side, tile_rows(t), group * 128:group * 128 + 128] = parts
+            return carry
+
+        lax.fori_loop(0, ROWS // 8, pack_y, 0)
+
+    def pack_rows_x(planes, at, xsend):
+        def pack_x(q, carry):
+            p = at(q)
+            for side in range(2):
+                start = TOP + ROWS - 8 if side == 0 else TOP
+                for group in range(3):
+                    parts = None
+                    for kind, c, width, place in PIECES[3 * group:3 * group + 3]:
+                        target = place - 8 * group
+                        piece = fields[kind][c, plane_of(kind, p), start:start + 8, LEFT:XCOLS]
+                        piece = roll(piece, target - (8 - width) if side == 0 else target, 0)
+                        parts = piece if parts is None else jnp.where(sub < target, parts, piece)
+                    xsend[side, q, 8 * group:8 * group + 8, :] = parts
+            return carry
+
+        lax.fori_loop(0, len(planes), pack_x, 0)
+
+    def exchange(stage, ysend, yrecv, xsend, xrecv):
+        plan = [
+            (xsend.at[0], xrecv.at[0], (x_up, gy)),
+            (xsend.at[1], xrecv.at[1], (x_down, gy)),
+        ]
+        for side, y in ((0, y_up), (1, y_down)):
+            plan += [
+                (ysend.at[side], yrecv.at[side, pl.ds(TOP, ROWS)], (gx, y)),
+                (ysend.at[side, pl.ds(ROWS - 8, 8)], yrecv.at[side, pl.ds(0, 8)], (x_up, y)),
+                (ysend.at[side, pl.ds(0, 8)], yrecv.at[side, pl.ds(TOP + ROWS, 8)], (x_down, y)),
+            ]
+        return [
+            pltpu.make_async_remote_copy(
+                src_ref=source, dst_ref=target,
+                send_sem=send_sem.at[stage, i], recv_sem=recv_sem.at[stage, i],
+                device_id=peer, device_id_type=MESH,
+            )
+            for i, (source, target, peer) in enumerate(plan)
+        ]
+
+    def unpack_rows_y(planes, yrecv):
+        def unpack_y(t, carry):
+            rows = tile_rows(t)
+            there = jnp.where(t == 0, has_down, jnp.where(t == 9, has_up, 1.0))
+            for group in range(2):
+                if not planes[5 * group:5 * group + 5]:
+                    continue
+                cols = pl.ds(group * 128, 128)
+                low = yrecv[0, rows, cols] * (there * has_left)
+                high = yrecv[1, rows, cols] * (there * has_right)
+                for i, p in enumerate(planes[5 * group:5 * group + 5]):
+                    for kind, c, width, place in PIECES:
+                        target = 24 * i + place
+                        piece = jnp.where(
+                            lane < 64, roll(high, -target, 1), roll(low, 128 - width - target, 1)
+                        )
+                        fields[kind].at[c, plane_of(kind, p)][rows, pl.ds(0, 128)] = piece
+            return carry
+
+        lax.fori_loop(0, XROWS // 8, unpack_y, 0)
+
+    def unpack_rows_x(planes, at, xrecv):
+        def unpack_x(q, carry):
+            p = at(q)
+            for side in range(2):
+                start = 0 if side == 0 else TOP + ROWS
+                for group in range(3):
+                    parts = xrecv[side, q, 8 * group:8 * group + 8, :]
+                    parts = parts * (has_down if side == 0 else has_up)
+                    for kind, c, width, place in PIECES[3 * group:3 * group + 3]:
+                        target = place - 8 * group
+                        shift = 8 - width - target if side == 0 else -target
+                        fields[kind][c, plane_of(kind, p), start:start + 8, LEFT:XCOLS] = roll(
+                            parts, shift, 0
+                        )
+            return carry
+
+        lax.fori_loop(0, len(planes), unpack_x, 0)
+
+    def ahead_x(tiles, t):
+        here = tiles[t]
+        if t < 9:
+            here = jnp.where(sub3 == 0, tiles[t + 1], here)
+        return pltpu.roll(here, 7, 0)
+
+    def behind_x(tiles, t):
+        here = tiles[t]
+        if t > 0:
+            here = jnp.where(sub3 == 7, tiles[t - 1], here)
+        return pltpu.roll(here, 1, 0)
+
+    def magnetic(start, stop):
+        def one(p, carry):
+            q = p + 1
+            eys = {0: elec[1, p, 0:8, :]}
+            ezs = {0: elec[2, p, 0:8, :]}
+            for t in range(10):
+                rows = slice(8 * t, 8 * t + 8)
+                if t < 9:
+                    eys[t + 1] = elec[1, p, 8 * t + 8:8 * t + 16, :]
+                    ezs[t + 1] = elec[2, p, 8 * t + 8:8 * t + 16, :]
+                ex, ey, ez = elec[0, p, rows, :], eys[t], ezs[t]
+                factor = corner if t == 0 else half
+                ez_y = pltpu.roll(ez, XCOLS - 1, 1)
+                ex_y = pltpu.roll(ex, XCOLS - 1, 1)
+                ez_x = ahead_x(ezs, t)
+                ey_x = ahead_x(eys, t)
+                magn[0, q, rows, :] -= factor * ((ez_y - ez) - (elec[1, q, rows, :] - ey))
+                magn[1, q, rows, :] -= factor * ((elec[0, q, rows, :] - ex) - (ez_x - ez))
+                magn[2, q, rows, :] -= factor * ((ey_x - ey) - (ex_y - ex))
+            return carry
+
+        lax.fori_loop(start, stop, one, 0)
+
+    def electric(start, stop):
+        def one(p, carry):
+            q = p + 1
+            hys, hzs = {}, {}
+            for t in range(10):
+                rows = slice(8 * t, 8 * t + 8)
+                hys[t] = magn[1, q, rows, :]
+                hzs[t] = magn[2, q, rows, :]
+                hx, hy, hz = magn[0, q, rows, :], hys[t], hzs[t]
+                hz_y = pltpu.roll(hz, 1, 1)
+                hx_y = pltpu.roll(hx, 1, 1)
+                hz_x = behind_x(hzs, t)
+                hy_x = behind_x(hys, t)
+                elec[0, p, rows, :] += (COURANT * perm[0, p, rows, :]) * (
+                    (hz - hz_y) - (hy - magn[1, p, rows, :])
+                )
+                elec[1, p, rows, :] += (COURANT * perm[1, p, rows, :]) * (
+                    (hx - magn[0, p, rows, :]) - (hz - hz_x)
+                )
+                elec[2, p, rows, :] += (COURANT * perm[2, p, rows, :]) * (
+                    (hy - hy_x) - (hx - hx_y)
+                )
+            return carry
+
+        lax.fori_loop(start, stop, one, 0)
+
+    for copy in loads_i:
+        copy.wait()
+    inner_at = lambda q: q + 3
+    outer_at = lambda q: q + 10 * (q // 3)
+    copies_i = exchange(0, ysend_i, yrecv_i, xsend_i, xrecv_i)
+    pack_rows_x(INNER, inner_at, xsend_i)
+    pl.semaphore_wait(barrier, len(greeted))
+    for copy in copies_i[:2]:
+        copy.start()
+    pack_rows_y(INNER, ysend_i)
+    for copy in copies_i[2:]:
+        copy.start()
+
+    for copy in loads_t:
+        copy.wait()
+
     for c in range(3):
         elec[c, NZ] = jnp.zeros((XROWS, XCOLS), F32)
         magn[c, 0] = jnp.zeros((XROWS, XCOLS), F32)
 
-    half = jnp.where((lanes >= 64) & (lanes < 128), COURANT * has_left, COURANT)
-    for t in range(10):
-        coef[8 * t:8 * t + 8, :] = half * has_down if t == 0 else half
-
+    place = lax.broadcasted_iota(jnp.int32, (16, 128), 0)
+    angle = jnp.zeros((16, 128), F32)
     for f in range(FREQ):
         for s in range(3):
-            angle = jnp.full((8, 128), freq_in[f] * (s + 1.0), F32)
-            trig[f, s, 0] = jnp.cos(angle)
-            trig[f, s, 1] = jnp.sin(angle)
+            angle = jnp.where(place == 3 * f + s, freq_in[f] * (s + 1.0), angle)
+    both = (jnp.cos(angle), jnp.sin(angle))
+    for f in range(FREQ):
+        for s in range(3):
+            k = 3 * f + s
+            for part in range(2):
+                trig[f, s, part] = jnp.broadcast_to(both[part][k:k + 1, :], (8, 128))
 
     col = gy * COLS + lax.broadcasted_iota(jnp.int32, (8, COLS), 1)
     inside = [
@@ -166,175 +357,19 @@
     used = lax.broadcasted_iota(jnp.int32, (n_x * CAP, 256), 1) < 3 * ROWS
     picker[...] = jnp.where((wanted == slots) & used, 1.0, 0.0).astype(jnp.bfloat16)
 
-    fields = (elec, magn, perm)
-
-    def plane_of(kind, p):
-        return p + 1 if kind == 1 else p
-
-    def pack(planes, at, ysend, xsend):
-        def pack_y(t, carry):
-            rows = pl.ds(pl.multiple_of(TOP + t * 8, 8), 8)
-            for side in range(2):
-                for group in range(2):
-                    parts = jnp.zeros((8, 128), F32)
-                    for i, p in enumerate(planes[5 * group:5 * group + 5]):
-                        for kind, c, width, place in PIECES:
-                            target = 24 * i + place
-                            ref = fields[kind].at[c, plane_of(kind, p)]
-                            if side == 0:
-                                piece = ref[rows, pl.ds(2 * 128, 128)]
-                                piece = roll(piece, target - (128 - width), 1)
-                            else:
-                                piece = ref[rows, pl.ds(128, 128)]
-                                piece = roll(piece, target, 1)
-                            parts = jnp.where(lane < target, parts, piece)
-                    ysend[side, tile_rows(t), group * 128:group * 128 + 128] = parts
-            return carry
-
-        lax.fori_loop(0, ROWS // 8, pack_y, 0)
-
-        def pack_x(q, carry):
-            p = at(q)
-            for side in range(2):
-                start = TOP + ROWS - 8 if side == 0 else TOP
-                for group in range(3):
-                    parts = None
-                    for kind, c, width, place in PIECES[3 * group:3 * group + 3]:
-                        target = place - 8 * group
-                        piece = fields[kind][c, plane_of(kind, p), start:start + 8, LEFT:XCOLS]
-                        piece = roll(piece, target - (8 - width) if side == 0 else target, 0)
-                        parts = piece if parts is None else jnp.where(sub < target, parts, piece)
-                    xsend[side, q, 8 * group:8 * group + 8, :] = parts
-            return carry
-
-        lax.fori_loop(0, len(planes), pack_x, 0)
-
-    def exchange(stage, ysend, yrecv, xsend, xrecv):
-        plan = [
-            (xsend.at[0], xrecv.at[0], (x_up, gy)),
-            (xsend.at[1], xrecv.at[1], (x_down, gy)),
-        ]
-        for side, y in ((0, y_up), (1, y_down)):
-            plan += [
-                (ysend.at[side], yrecv.at[side, pl.ds(TOP, ROWS)], (gx, y)),
-                (ysend.at[side, pl.ds(ROWS - 8, 8)], yrecv.at[side, pl.ds(0, 8)], (x_up, y)),
-                (ysend.at[side, pl.ds(0, 8)], yrecv.at[side, pl.ds(TOP + ROWS, 8)], (x_down, y)),
-            ]
-        return [
-            pltpu.make_async_remote_copy(
-                src_ref=source, dst_ref=target,
-                send_sem=send_sem.at[stage, i], recv_sem=recv_sem.at[stage, i],
-                device_id=peer, device_id_type=MESH,
-            )
-            for i, (source, target, peer) in enumerate(plan)
-        ]
-
-    def unpack(planes, at, yrecv, xrecv):
-        def unpack_y(t, carry):
-            rows = tile_rows(t)
-            there = jnp.where(t == 0, has_down, jnp.where(t == 9, has_up, 1.0))
-            for group in range(2):
-                if not planes[5 * group:5 * group + 5]:
-                    continue
-                cols = pl.ds(group * 128, 128)
-                low = yrecv[0, rows, cols] * (there * has_left)
-                high = yrecv[1, rows, cols] * (there * has_right)
-                for i, p in enumerate(planes[5 * group:5 * group + 5]):
-                    for kind, c, width, place in PIECES:
-                        target = 24 * i + place
-                        piece = jnp.where(
-                            lane < 64, roll(high, -target, 1), roll(low, 128 - width - target, 1)
-                        )
-                        fields[kind].at[c, plane_of(kind, p)][rows, pl.ds(0, 128)] = piece
-            return carry
-
-        lax.fori_loop(0, XROWS // 8, unpack_y, 0)
-
-        def unpack_x(q, carry):
-            p = at(q)
-            for side in range(2):
-                start = 0 if side == 0 else TOP + ROWS
-                for group in range(3):
-                    parts = xrecv[side, q, 8 * group:8 * group + 8, :]
-                    parts = parts * (has_down if side == 0 else has_up)
-                    for kind, c, width, place in PIECES[3 * group:3 * group + 3]:
-                        target = place - 8 * group
-                        shift = 8 - width - target if side == 0 else -target
-                        fields[kind][c, plane_of(kind, p), start:start + 8, LEFT:XCOLS] = roll(
-                            parts, shift, 0
-                        )
-            return carry
-
-        lax.fori_loop(0, len(planes), unpack_x, 0)
-
-    def ahead_x(ref, c, p, t, value):
-        if t == 9:
-            return pltpu.roll(value, 7, 0)
-        return pltpu.roll(jnp.where(sub3 == 0, ref[c, p, 8 * t + 8:8 * t + 16, :], value), 7, 0)
-
-    def behind_x(ref, c, p, t, value):
-        if t == 0:
-            return pltpu.roll(value, 1, 0)
-        return pltpu.roll(jnp.where(sub3 == 7, ref[c, p, 8 * t - 8:8 * t, :], value), 1, 0)
-
-    def magnetic(start, stop):
-        def one(p, carry):
-            for t in range(10):
-                rows = slice(8 * t, 8 * t + 8)
-                ex, ey, ez = (elec[c, p, rows, :] for c in range(3))
-                factor = coef[rows, :]
-                ez_y = pltpu.roll(ez, XCOLS - 1, 1)
-                ex_y = pltpu.roll(ex, XCOLS - 1, 1)
-                ez_x = ahead_x(elec, 2, p, t, ez)
-                ey_x = ahead_x(elec, 1, p, t, ey)
-                q = p + 1
-                magn[0, q, rows, :] -= factor * ((ez_y - ez) - (elec[1, q, rows, :] - ey))
-                magn[1, q, rows, :] -= factor * ((elec[0, q, rows, :] - ex) - (ez_x - ez))
-                magn[2, q, rows, :] -= factor * ((ey_x - ey) - (ex_y - ex))
-            return carry
-
-        lax.fori_loop(start, stop, one, 0)
-
-    def electric(start, stop):
-        def one(p, carry):
-            for t in range(10):
-                rows = slice(8 * t, 8 * t + 8)
-                q = p + 1
-                hx, hy, hz = (magn[c, q, rows, :] for c in range(3))
-                hz_y = pltpu.roll(hz, 1, 1)
-                hx_y = pltpu.roll(hx, 1, 1)
-                hz_x = behind_x(magn, 2, q, t, hz)
-                hy_x = behind_x(magn, 1, q, t, hy)
-                elec[0, p, rows, :] += (COURANT * perm[0, p, rows, :]) * (
-                    (hz - hz_y) - (hy - magn[1, p, rows, :])
-                )
-                elec[1, p, rows, :] += (COURANT * perm[1, p, rows, :]) * (
-                    (hx - magn[0, p, rows, :]) - (hz - hz_x)
-                )
-                elec[2, p, rows, :] += (COURANT * perm[2, p, rows, :]) * (
-                    (hy - hy_x) - (hx - hx_y)
-                )
-            return carry
-
-        lax.fori_loop(start, stop, one, 0)
-
-    for copy in loads_i:
-        copy.wait()
-    pack(INNER, lambda q: q + 3, ysend_i, xsend_i)
-    pl.semaphore_wait(barrier, len(greeted))
-    copies_i = exchange(0, ysend_i, yrecv_i, xsend_i, xrecv_i)
-    for copy in copies_i:
-        copy.start()
     for copy in loads_o:
         copy.wait()
-    outer_at = lambda q: q + 10 * (q // 3)
-    pack(OUTER, outer_at, ysend_o, xsend_o)
-    for copy in copies_i:
+    pack_rows_x(OUTER, outer_at, xsend_o)
+    pack_rows_y(OUTER, ysend_o)
+    for copy in copies_i[:2]:
+        copy.wait()
+    unpack_rows_x(INNER, inner_at, xrecv_i)
+    for copy in copies_i[2:]:
         copy.wait()
     copies_o = exchange(1, ysend_o, yrecv_o, xsend_o, xrecv_o)
     for copy in copies_o:
         copy.start()
-    unpack(INNER, lambda q: q + 3, yrecv_i, xrecv_i)
+    unpack_rows_y(INNER, yrecv_i)
 
     for s in range(3):
         magnetic(3 + s, 12 - s)
@@ -376,8 +411,8 @@
 
     lax.fori_loop(0, DP * 8, gradient, 0)
 
-    def edges_y(t, carry):
-        ext = pl.ds(pl.multiple_of(TOP + t * 8, 8), 8)
+    for t in range(ROWS // 8):
+        ext = slice(TOP + t * 8, TOP + t * 8 + 8)
         for side in range(2):
             parts = jnp.zeros((8, 128), F32)
             for m in range(FREQ * DP):
@@ -386,12 +421,8 @@
                 else:
                     piece = roll(masked[m, ext, 128:256], 3 * m, 1)
                 parts = jnp.where(lane < 3 * m, parts, piece)
-            ysend_m[side, tile_rows(t), :] = parts
-        return carry
-
-    lax.fori_loop(0, ROWS // 8, edges_y, 0)
-
-    def edges_x(j, carry):
+            ysend_m[side, 8 * t:8 * t + 8, :] = parts
+    for j in range(FREQ * DP // 2):
         for side in range(2):
             start = TOP + ROWS - 8 if side == 0 else TOP
             first = masked[2 * j, start:start + 8, LEFT:XCOLS]
@@ -400,11 +431,7 @@
                 parts = jnp.where(sub < 3, second, first)
             else:
                 parts = jnp.where(sub < 3, first, second)
-            xsend_m[side, tile_rows(j), :] = parts
-        return carry
-
-    lax.fori_loop(0, FREQ * DP // 2, edges_x, 0)
-
+            xsend_m[side, 8 * j:8 * j + 8, :] = parts
     copies_m = exchange(2, ysend_m, yrecv_m, xsend_m, xrecv_m)
     for copy in copies_m:
         copy.start()
@@ -489,46 +516,50 @@
 
     for copy in copies_o:
         copy.wait()
-    unpack(OUTER, outer_at, yrecv_o, xrecv_o)
+    unpack_rows_x(OUTER, outer_at, xrecv_o)
+    unpack_rows_y(OUTER, yrecv_o)
     for s in range(3):
         magnetic(12 - s, NZ)
         magnetic(0, 3 + s)
         electric(12 - s, NZ)
         electric(0, 4 + s)
-    saves = [
-        pltpu.make_async_copy(elec.at[:, pl.ds(0, NZ), own_r, own_c], elec_out, save_sem.at[0]),
-        pltpu.make_async_copy(magn.at[:, pl.ds(1, NZ), own_r, own_c], magn_out, save_sem.at[1]),
+    for copy in routes:
+        copy.wait()
+
+
+def save(elec, magn, owned, elec_out, magn_out, owned_out, sem):
+    own_r, own_c = pl.ds(TOP, ROWS), pl.ds(LEFT, COLS)
+    copies = [
+        pltpu.make_async_copy(elec.at[:, pl.ds(0, NZ), own_r, own_c], elec_out, sem.at[0]),
+        pltpu.make_async_copy(magn.at[:, pl.ds(1, NZ), own_r, own_c], magn_out, sem.at[1]),
+        pltpu.make_async_copy(owned, owned_out, sem.at[2]),
     ]
-    for copy in saves:
-        copy.start()
-    for copy in routes:
-        copy.wait()
-    for copy in saves:
+    for copy in copies:
+        copy.start()
+    for copy in copies:
         copy.wait()
 
 
 def body(n_x, n_y, elec, magn, perm, spec, freq, mask, owner):
-    any_space = pl.BlockSpec(memory_space=pl.ANY)
+    hbm = pl.BlockSpec(memory_space=pltpu.HBM)
     vmem = pl.BlockSpec(memory_space=pltpu.VMEM)
-    smem = pl.BlockSpec(memory_space=pltpu.SMEM)
     buf = pltpu.VMEM
     sem = pltpu.SemaphoreType.DMA
-    return pl.pallas_call(
+    held = pl.pallas_call(
         functools.partial(kernel, n_x, n_y),
         out_shape=(
-            jax.ShapeDtypeStruct((3, NZ, ROWS, COLS), F32),
-            jax.ShapeDtypeStruct((3, NZ, ROWS, COLS), F32),
-            jax.ShapeDtypeStruct((FREQ, DP, n_x * CAP, COLS), F32),
-        ),
-        in_specs=[any_space] * 4 + [smem, any_space, vmem],
-        out_specs=(OUT_SPACE, OUT_SPACE, OUT_SPACE),
-        scratch_shapes=[
             buf((3, NZ + 1, XROWS, XCOLS), F32),
             buf((3, NZ + 1, XROWS, XCOLS), F32),
+            buf((FREQ, DP, n_x * CAP, COLS), F32),
+        ),
+        in_specs=[hbm] * 7,
+        out_specs=(vmem, vmem, vmem),
+        scratch_shapes=[
             buf((3, NZ, XROWS, XCOLS), F32),
             buf((FREQ, 2, 3, DP, ROWS, COLS), F32),
+            pltpu.SMEM((FREQ,), F32),
             buf((DP, ROWS, COLS), jnp.int32),
-            buf((XROWS, XCOLS), F32),
+            buf((8, 128), jnp.int32),
             buf((FREQ, 3, 2, 8, 128), F32),
             buf((2, 3, DP, ROWS, COLS), F32),
             buf((FREQ * DP, XROWS, XCOLS), F32),
@@ -543,17 +574,27 @@
             buf((2, len(OUTER), 24, COLS), F32), buf((2, len(OUTER), 24, COLS), F32),
             buf((2, ROWS, 128), F32), buf((2, XROWS, 128), F32),
             buf((2, ROWS, COLS), F32), buf((2, ROWS, COLS), F32),
-            sem((11,)), sem((2,)), sem((FREQ,)), sem((3, 8)), sem((3, 8)),
+            sem((13,)), sem((FREQ,)), sem((3, 8)), sem((3, 8)),
             sem((FREQ, n_x)), sem((FREQ, n_x)),
         ],
         compiler_params=pltpu.CompilerParams(
-            collective_id=0, has_side_effects=True, vmem_limit_bytes=52 << 20
+            collective_id=0, has_side_effects=True, vmem_limit_bytes=36 << 20
         ),
         name="adjoint",
-    )(elec, magn, perm, spec, freq, mask, owner.reshape(8, 128))
-
-
-OUT_SPACE = pl.BlockSpec(memory_space=pl.ANY)
+    )(*[pltpu.with_memory_space_constraint(v, pltpu.HBM) for v in (elec, magn, perm, spec, freq, mask, owner.reshape(8, 128))])
+    return pl.pallas_call(
+        save,
+        out_shape=(
+            jax.ShapeDtypeStruct((3, NZ, ROWS, COLS), F32),
+            jax.ShapeDtypeStruct((3, NZ, ROWS, COLS), F32),
+            jax.ShapeDtypeStruct((FREQ, DP, n_x * CAP, COLS), F32),
+        ),
+        in_specs=[vmem] * 3,
+        out_specs=(hbm,) * 3,
+        scratch_shapes=[sem((3,))],
+        compiler_params=pltpu.CompilerParams(vmem_limit_bytes=1 << 20),
+        name="save",
+    )(*held)
 
 
 def solution(mesh):

time: 77.8 us -> 72.2 us (0.928)
  local copies, waits for them, and re-layouts: 10.4 us -> 0 us
  Pallas kernels: 66.5 us -> 71.4 us
    unnamed x13 -> x0, local copies, waits for them, and re-layouts: 10.4 us -> none
    pallas_call x1 -> x2, Pallas kernels: 66.5 us -> 71.4 us  [the longest x1 68 us: body(): pl.pallas_call(functools.partial(kernel, n_x, n_y), out_shape=(buf((3, NZ...]
where the time goes in v2:
time: 72.2 us; the launch traced here: 72 us
  Pallas kernels  71.4 us (99%)
    pallas_call x1, Pallas kernels, body(): pl.pallas_call(functools.partial(kernel, n_x, n_y), out_shape=(buf((3, NZ...  68 us
    pallas_call x1, Pallas kernels, body(): pl.pallas_call(save, out_shape=(jax.ShapeDtypeStruct((3, NZ, ROWS, COLS),...  3.42 us

profile of v2, /device:TPU:1, one launch (start us, length us, event | category | flops | bytes accessed | tf_op | source)
XLA Modules:
  0.0 72.0 jit_solution(1956532875143384423)
XLA Ops:
  0.6 68.0 %adjoint.1 = (f32[3,17,80,384]{3,2,1,0:T(8,128)S(1)}, f32[3,17,80,384]{3,2,1,0:T(8,128)S(1)}, f32[4,4,128,256]{3,2,1,0:T(8,128)S(1)}) custom-call(f32[3,16,64,256]{3,2,1,0:T(8,128)} %elec_in.1, f32[3,16,64,256]{3,2,1,0:T(8,128)} %magn_in.1, f32[3,16,64,256]{3,2,1,0:T(8,128)} %perm_in.1, f32[4,2,3,4,64,256]{5,4,3,2,1,0:T(8,128)} %spec_in.1, f32[4]{0:T(128)} %freq_hbm.1, ...), custom_call_target="tpu_custom_call" | custom-call | tf_op jit(solution)/shard_map/adjoint/pallas_call | solution.py:548
  68.6 3.4 %save.1 = (f32[3,16,64,256]{3,2,1,0:T(8,128)}, f32[3,16,64,256]{3,2,1,0:T(8,128)}, f32[4,4,128,256]{3,2,1,0:T(8,128)}) custom-call(f32[3,17,80,384]{3,2,1,0:T(8,128)S(1)} %get-tuple-element.6.elec, f32[3,17,80,384]{3,2,1,0:T(8,128)S(1)} %get-tuple-element.7.magn, f32[4,4,128,256]{3,2,1,0:T(8,128)S(1)} %get-tuple-element.8.owned), custom_call_target="tpu_custom_call" | custom-call | tf_op jit(solution)/shard_map/save/pallas_call | solution.py:585

commit v3 on v2

--- a/solution.py
+++ b/solution.py
@@ -50,18 +50,24 @@
 def kernel(
     n_x, n_y,
     elec_in, magn_in, perm_in, spec_in, freq_hbm, mask_in, owner_hbm,
-    elec, magn, owned_out,
-    perm, spec, freq_in, mask, owner_in, trig, early, masked, inverse_norm, picker,
-    fold, plane_out, packed,
+    elec_out, magn_out, owned_out,
+    elec, magn, perm, spec, freq_in, mask, owner_in, trig, early, masked, inverse_norm, picker,
+    fold, plane_out, packed, landed,
     ysend_i, yrecv_i, xsend_i, xrecv_i,
     ysend_o, yrecv_o, xsend_o, xrecv_o,
     ysend_m, yrecv_m, xsend_m, xrecv_m,
-    load_sem, own_sem, send_sem, recv_sem, route_send, route_recv,
+    load_sem, save_sem, send_sem, recv_sem, route_sem,
 ):
     gx = lax.axis_index("gx")
     gy = lax.axis_index("gy")
     x_up, x_down = lax.rem(gx + 1, n_x), lax.rem(gx + n_x - 1, n_x)
     y_up, y_down = lax.rem(gy + 1, n_y), lax.rem(gy + n_y - 1, n_y)
+
+    barrier = pltpu.get_barrier_semaphore()
+    greeted = [(lax.rem(gx + k, n_x), gy) for k in range(1, n_x)]
+    greeted += [(x, y) for x in (x_down, gx, x_up) for y in (y_down, y_up)]
+    for peer in greeted:
+        pl.semaphore_signal(barrier, inc=1, device_id=peer, device_id_type=MESH)
 
     own_r, own_c = pl.ds(TOP, ROWS), pl.ds(LEFT, COLS)
 
@@ -78,17 +84,17 @@
         load(perm_in, perm, 3, 10, 0, 2),
     ]
     loads_o = [
-        load(elec_in, elec, 0, 3, 0, 3), load(elec_in, elec, 13, 3, 0, 4),
-        load(magn_in, magn, 0, 3, 1, 5), load(magn_in, magn, 13, 3, 1, 6),
-        load(perm_in, perm, 0, 3, 0, 7), load(perm_in, perm, 13, 3, 0, 8),
+        load(elec_in, elec, 0, 3, 0, 3), load(elec_in, elec, 13, 3, 0, 3),
+        load(magn_in, magn, 0, 3, 1, 4), load(magn_in, magn, 13, 3, 1, 4),
+        load(perm_in, perm, 0, 3, 0, 5), load(perm_in, perm, 13, 3, 0, 5),
     ]
     loads_s = [
-        pltpu.make_async_copy(spec_in, spec, load_sem.at[9]),
-        pltpu.make_async_copy(mask_in, mask, load_sem.at[10]),
+        pltpu.make_async_copy(spec_in, spec, load_sem.at[6]),
+        pltpu.make_async_copy(mask_in, mask, load_sem.at[7]),
     ]
     loads_t = [
-        pltpu.make_async_copy(freq_hbm, freq_in, load_sem.at[11]),
-        pltpu.make_async_copy(owner_hbm, owner_in, load_sem.at[12]),
+        pltpu.make_async_copy(freq_hbm, freq_in, load_sem.at[8]),
+        pltpu.make_async_copy(owner_hbm, owner_in, load_sem.at[9]),
     ]
     for copy in loads_t:
         copy.start()
@@ -98,12 +104,6 @@
         copy.start()
     for copy in loads_s:
         copy.start()
-
-    barrier = pltpu.get_barrier_semaphore()
-    greeted = [(lax.rem(gx + k, n_x), gy) for k in range(1, n_x)]
-    greeted += [(x, y) for x in (x_down, gx, x_up) for y in (y_down, y_up)]
-    for peer in greeted:
-        pl.semaphore_signal(barrier, inc=1, device_id=peer, device_id_type=MESH)
 
     lane = lax.broadcasted_iota(jnp.int32, (8, 128), 1)
     lanes = lax.broadcasted_iota(jnp.int32, (8, XCOLS), 1)
@@ -161,25 +161,34 @@
 
         lax.fori_loop(0, len(planes), pack_x, 0)
 
-    def exchange(stage, ysend, yrecv, xsend, xrecv):
+    def exchange(stage, ysend, yrecv, xsend, xrecv, top, count):
         plan = [
             (xsend.at[0], xrecv.at[0], (x_up, gy)),
             (xsend.at[1], xrecv.at[1], (x_down, gy)),
         ]
         for side, y in ((0, y_up), (1, y_down)):
             plan += [
-                (ysend.at[side], yrecv.at[side, pl.ds(TOP, ROWS)], (gx, y)),
-                (ysend.at[side, pl.ds(ROWS - 8, 8)], yrecv.at[side, pl.ds(0, 8)], (x_up, y)),
-                (ysend.at[side, pl.ds(0, 8)], yrecv.at[side, pl.ds(TOP + ROWS, 8)], (x_down, y)),
+                (ysend.at[side], yrecv.at[side, pl.ds(top, count)], (gx, y)),
+                (ysend.at[side, pl.ds(count - 8, 8)], yrecv.at[side, pl.ds(0, 8)], (x_up, y)),
+                (ysend.at[side, pl.ds(0, 8)], yrecv.at[side, pl.ds(top + count, 8)], (x_down, y)),
             ]
         return [
             pltpu.make_async_remote_copy(
                 src_ref=source, dst_ref=target,
-                send_sem=send_sem.at[stage, i], recv_sem=recv_sem.at[stage, i],
+                send_sem=send_sem.at[stage, min(i // 2, 1)],
+                recv_sem=recv_sem.at[stage, min(i // 2, 1)],
                 device_id=peer, device_id_type=MESH,
             )
             for i, (source, target, peer) in enumerate(plan)
         ]
+
+    def finish(stage, kind, buffer):
+        copy = pltpu.make_async_remote_copy(
+            src_ref=buffer, dst_ref=buffer,
+            send_sem=send_sem.at[stage, kind], recv_sem=recv_sem.at[stage, kind],
+            device_id=(x_up, gy), device_id_type=MESH,
+        )
+        copy.wait()
 
     def unpack_rows_y(planes, yrecv):
         def unpack_y(t, carry):
@@ -285,7 +294,7 @@
         copy.wait()
     inner_at = lambda q: q + 3
     outer_at = lambda q: q + 10 * (q // 3)
-    copies_i = exchange(0, ysend_i, yrecv_i, xsend_i, xrecv_i)
+    copies_i = exchange(0, ysend_i, yrecv_i, xsend_i, xrecv_i, TOP, ROWS)
     pack_rows_x(INNER, inner_at, xsend_i)
     pl.semaphore_wait(barrier, len(greeted))
     for copy in copies_i[:2]:
@@ -357,33 +366,25 @@
     used = lax.broadcasted_iota(jnp.int32, (n_x * CAP, 256), 1) < 3 * ROWS
     picker[...] = jnp.where((wanted == slots) & used, 1.0, 0.0).astype(jnp.bfloat16)
 
-    for copy in loads_o:
-        copy.wait()
+    for k, (source, target) in enumerate(((elec_in, elec), (magn_in, magn), (perm_in, perm))):
+        load(source, target, 0, 6, 0, 3 + k).wait()
     pack_rows_x(OUTER, outer_at, xsend_o)
     pack_rows_y(OUTER, ysend_o)
-    for copy in copies_i[:2]:
-        copy.wait()
+    finish(0, 0, xrecv_i)
     unpack_rows_x(INNER, inner_at, xrecv_i)
-    for copy in copies_i[2:]:
-        copy.wait()
-    copies_o = exchange(1, ysend_o, yrecv_o, xsend_o, xrecv_o)
+    finish(0, 1, yrecv_i)
+    copies_o = exchange(1, ysend_o, yrecv_o, xsend_o, xrecv_o, TOP, ROWS)
     for copy in copies_o:
         copy.start()
     unpack_rows_y(INNER, yrecv_i)
 
-    for s in range(3):
-        magnetic(3 + s, 12 - s)
-        electric(4 + s, 12 - s)
-        if s < 2:
-            def keep_plane(p, carry, s=s):
-                for c in range(3):
-                    early[s, c, p] = elec[c, FIRST + p, TOP:TOP + ROWS, LEFT:XCOLS]
-                return carry
-
-            lax.fori_loop(0, DP, keep_plane, 0)
-
-    for copy in loads_s:
-        copy.wait()
+    def keep_planes(s, start, stop):
+        def keep_plane(p, carry):
+            for c in range(3):
+                early[s, c, p] = elec[c, FIRST + p, TOP:TOP + ROWS, LEFT:XCOLS]
+            return carry
+
+        lax.fori_loop(start, stop, keep_plane, 0)
 
     def gradient(k, carry):
         p, t = k // 8, lax.rem(k, 8)
@@ -406,116 +407,140 @@
                         total = total + spec[f, part, c, p, rows, cols] * (
                             w1 * e1 + w2 * e2 + w3 * e3
                         )
-                masked[f * DP + p, ext, far] = total * keep
+                masked[p * FREQ + f, ext, far] = total * keep
         return carry
 
-    lax.fori_loop(0, DP * 8, gradient, 0)
-
-    for t in range(ROWS // 8):
-        ext = slice(TOP + t * 8, TOP + t * 8 + 8)
+    def send_edges(part):
+        lax.fori_loop(part * 16, part * 16 + 16, gradient, 0)
         for side in range(2):
-            parts = jnp.zeros((8, 128), F32)
-            for m in range(FREQ * DP):
+            for odd in range(2):
+                parts = jnp.zeros((8, 128), F32)
+                for group in range(4):
+                    t = 2 * group + odd
+                    ext = slice(TOP + t * 8, TOP + t * 8 + 8)
+                    for q in range(8):
+                        m, target = part * 8 + q, 32 * group + 3 * q
+                        if side == 0:
+                            piece = roll(masked[m, ext, 256:384], target + 3, 1)
+                        else:
+                            piece = roll(masked[m, ext, 128:256], target, 1)
+                        parts = jnp.where(lane < target, parts, piece)
+                ysend_m[part, side, 8 * odd:8 * odd + 8, :] = parts
+            for j in range(4):
+                start = TOP + ROWS - 8 if side == 0 else TOP
+                m = part * 8 + 2 * j
+                first = masked[m, start:start + 8, LEFT:XCOLS]
+                second = pltpu.roll(masked[m + 1, start:start + 8, LEFT:XCOLS], 3, 0)
                 if side == 0:
-                    piece = roll(masked[m, ext, 256:384], 3 * m + 3, 1)
+                    parts = jnp.where(sub < 3, second, first)
                 else:
-                    piece = roll(masked[m, ext, 128:256], 3 * m, 1)
-                parts = jnp.where(lane < 3 * m, parts, piece)
-            ysend_m[side, 8 * t:8 * t + 8, :] = parts
-    for j in range(FREQ * DP // 2):
-        for side in range(2):
-            start = TOP + ROWS - 8 if side == 0 else TOP
-            first = masked[2 * j, start:start + 8, LEFT:XCOLS]
-            second = pltpu.roll(masked[2 * j + 1, start:start + 8, LEFT:XCOLS], 3, 0)
-            if side == 0:
-                parts = jnp.where(sub < 3, second, first)
-            else:
-                parts = jnp.where(sub < 3, first, second)
-            xsend_m[side, 8 * j:8 * j + 8, :] = parts
-    copies_m = exchange(2, ysend_m, yrecv_m, xsend_m, xrecv_m)
-    for copy in copies_m:
-        copy.start()
-    for copy in copies_m:
-        copy.wait()
-
-    def put_y(t, carry):
-        rows = tile_rows(t)
-        there = jnp.where(t == 0, has_down, jnp.where(t == 9, has_up, 1.0))
-        low = yrecv_m[0, rows, :] * (there * has_left)
-        high = yrecv_m[1, rows, :] * (there * has_right)
-        for m in range(FREQ * DP):
-            masked[m, rows, 0:128] = jnp.where(
-                lane < 64, roll(high, -3 * m, 1), roll(low, 125 - 3 * m, 1)
-            )
-        return carry
-
-    lax.fori_loop(0, XROWS // 8, put_y, 0)
-
-    def put_x(j, carry):
+                    parts = jnp.where(sub < 3, first, second)
+                xsend_m[part, side, 8 * j:8 * j + 8, :] = parts
+        for copy in exchange(
+            2 + part, ysend_m.at[part], yrecv_m.at[part], xsend_m.at[part], xrecv_m.at[part], 8, 16
+        ):
+            copy.start()
+
+    def put_edges(part):
+        finish(2 + part, 0, xrecv_m.at[part])
         for side in range(2):
             start = 0 if side == 0 else TOP + ROWS
-            parts = xrecv_m[side, tile_rows(j), :] * (has_down if side == 0 else has_up)
-            masked[2 * j, start:start + 8, LEFT:XCOLS] = parts
-            masked[2 * j + 1, start:start + 8, LEFT:XCOLS] = pltpu.roll(parts, 5, 0)
+            for j in range(4):
+                m = part * 8 + 2 * j
+                parts = xrecv_m[part, side, 8 * j:8 * j + 8, :]
+                parts = parts * (has_down if side == 0 else has_up)
+                masked[m, start:start + 8, LEFT:XCOLS] = parts
+                masked[m + 1, start:start + 8, LEFT:XCOLS] = pltpu.roll(parts, 5, 0)
+        finish(2 + part, 1, yrecv_m.at[part])
+        for t in range(10):
+            if t == 0:
+                there, row, shift = has_down, 0, 96
+            elif t == 9:
+                there, row, shift = has_up, 24, 0
+            else:
+                there, row, shift = 1.0, 8 + 8 * ((t - 1) % 2), 32 * ((t - 1) // 2)
+            low = yrecv_m[part, 0, row:row + 8, :] * (there * has_left)
+            high = yrecv_m[part, 1, row:row + 8, :] * (there * has_right)
+            for q in range(8):
+                target = shift + 3 * q
+                masked[part * 8 + q, 8 * t:8 * t + 8, 0:128] = jnp.where(
+                    lane < 64, roll(high, -target, 1), roll(low, 125 - target, 1)
+                )
+
+    magnetic(3, 10)
+    electric(4, 10)
+    keep_planes(0, 0, DP)
+    magnetic(4, 9)
+    electric(5, 9)
+    keep_planes(1, 0, 3)
+    magnetic(5, 8)
+    electric(6, 8)
+    for copy in loads_s:
+        copy.wait()
+    send_edges(0)
+    magnetic(10, 12)
+    electric(10, 12)
+    magnetic(9, 11)
+    electric(9, 11)
+    keep_planes(1, 3, DP)
+    magnetic(8, 10)
+    electric(8, 10)
+    send_edges(1)
+
+    def filter_plane(m, carry):
+        for t in range(10):
+            value = masked[m, 8 * t:8 * t + 8, :]
+            center = value[:, LEFT:XCOLS]
+            pairs = [
+                (pltpu.roll(value, b, 1) + pltpu.roll(value, XCOLS - b, 1))[:, LEFT:XCOLS]
+                for b in range(1, RADIUS + 1)
+            ]
+            for a in range(RADIUS + 1):
+                if a == 0 and t in (0, 9):
+                    continue
+                total = weight(a, 0) * center
+                for b in range(1, RADIUS + 1):
+                    if weight(a, b) > 0.0:
+                        total = total + weight(a, b) * pairs[b - 1]
+                fold[a, 8 * t:8 * t + 8, :] = total
+        for t in range(1, 9):
+            total = fold[0, 8 * t:8 * t + 8, :]
+            for a in range(1, RADIUS + 1):
+                here = fold[a, 8 * t:8 * t + 8, :]
+                after = fold[a, 8 * t + 8:8 * t + 16, :]
+                before = fold[a, 8 * t - 8:8 * t, :]
+                total = total + pltpu.roll(jnp.where(sub < a, after, here), 8 - a, 0)
+                total = total + pltpu.roll(jnp.where(sub >= 8 - a, before, here), a, 0)
+            plane_out[8 * t - 8:8 * t, :] = total * inverse_norm[8 * t - 8:8 * t, :]
+        value = plane_out[...]
+        high = value.astype(jnp.bfloat16)
+        rest = value - high.astype(F32)
+        middle = rest.astype(jnp.bfloat16)
+        low = (rest - middle.astype(F32)).astype(jnp.bfloat16)
+        stacked = jnp.concatenate([high, middle, low, jnp.zeros_like(low)], axis=0)
+        picked = jnp.dot(picker[...], stacked, preferred_element_type=F32)
+        packed[lax.rem(m, FREQ), m // FREQ] = picked
         return carry
 
-    lax.fori_loop(0, FREQ * DP // 2, put_x, 0)
-
-    routes = []
-    for f in range(FREQ):
-        def filter_plane(p, carry, f=f):
-            m = f * DP + p
-            for t in range(10):
-                value = masked[m, 8 * t:8 * t + 8, :]
-                center = value[:, LEFT:XCOLS]
-                pairs = [
-                    (pltpu.roll(value, b, 1) + pltpu.roll(value, XCOLS - b, 1))[:, LEFT:XCOLS]
-                    for b in range(1, RADIUS + 1)
-                ]
-                for a in range(RADIUS + 1):
-                    if a == 0 and t in (0, 9):
-                        continue
-                    total = weight(a, 0) * center
-                    for b in range(1, RADIUS + 1):
-                        if weight(a, b) > 0.0:
-                            total = total + weight(a, b) * pairs[b - 1]
-                    fold[a, 8 * t:8 * t + 8, :] = total
-            for t in range(1, 9):
-                total = fold[0, 8 * t:8 * t + 8, :]
-                for a in range(1, RADIUS + 1):
-                    here = fold[a, 8 * t:8 * t + 8, :]
-                    after = fold[a, 8 * t + 8:8 * t + 16, :]
-                    before = fold[a, 8 * t - 8:8 * t, :]
-                    total = total + pltpu.roll(jnp.where(sub < a, after, here), 8 - a, 0)
-                    total = total + pltpu.roll(jnp.where(sub >= 8 - a, before, here), a, 0)
-                plane_out[8 * t - 8:8 * t, :] = total * inverse_norm[8 * t - 8:8 * t, :]
-            value = plane_out[...]
-            high = value.astype(jnp.bfloat16)
-            rest = value - high.astype(F32)
-            middle = rest.astype(jnp.bfloat16)
-            low = (rest - middle.astype(F32)).astype(jnp.bfloat16)
-            stacked = jnp.concatenate([high, middle, low, jnp.zeros_like(low)], axis=0)
-            packed[f, p] = jnp.dot(picker[...], stacked, preferred_element_type=F32)
-            return carry
-
-        lax.fori_loop(0, DP, filter_plane, 0)
-        mine = pl.ds(pl.multiple_of(gx * CAP, CAP), CAP)
+    mine = pl.ds(pl.multiple_of(gx * CAP, CAP), CAP)
+    for p in range(DP):
+        if p % 2 == 0:
+            put_edges(p // 2)
+        lax.fori_loop(p * FREQ, p * FREQ + FREQ, filter_plane, 0)
         for k in list(range(n_x // 2, n_x)) + list(range(1, n_x // 2)):
             owner = gx ^ k
             theirs = pl.ds(pl.multiple_of(owner * CAP, CAP), CAP)
-            copy = pltpu.make_async_remote_copy(
-                src_ref=packed.at[f, :, theirs], dst_ref=owned_out.at[f, :, mine],
-                send_sem=route_send.at[f, k], recv_sem=route_recv.at[f, k],
+            pltpu.make_async_remote_copy(
+                src_ref=packed.at[:, p, theirs], dst_ref=landed.at[:, p, mine],
+                send_sem=route_sem.at[0], recv_sem=route_sem.at[1],
                 device_id=(owner, gy), device_id_type=MESH,
-            )
-            copy.start()
-            routes.append(copy)
-        copy = pltpu.make_async_copy(packed.at[f, :, mine], owned_out.at[f, :, mine], own_sem.at[f])
-        copy.start()
-        routes.append(copy)
-
-    for copy in copies_o:
-        copy.wait()
+            ).start()
+        pltpu.make_async_copy(
+            packed.at[:, p, mine], landed.at[:, p, mine], route_sem.at[2]
+        ).start()
+
+    finish(1, 0, xrecv_o)
+    finish(1, 1, yrecv_o)
     unpack_rows_x(OUTER, outer_at, xrecv_o)
     unpack_rows_y(OUTER, yrecv_o)
     for s in range(3):
@@ -523,15 +548,31 @@
         magnetic(0, 3 + s)
         electric(12 - s, NZ)
         electric(0, 4 + s)
-    for copy in routes:
+    saves = [
+        pltpu.make_async_copy(elec.at[:, pl.ds(0, NZ), own_r, own_c], elec_out, save_sem.at[0]),
+        pltpu.make_async_copy(magn.at[:, pl.ds(1, NZ), own_r, own_c], magn_out, save_sem.at[1]),
+    ]
+    for copy in saves:
+        copy.start()
+    for copy in saves:
         copy.wait()
+    others = pl.ds(0, (n_x - 1) * CAP)
+    pltpu.make_async_remote_copy(
+        src_ref=packed.at[:, :, others], dst_ref=landed.at[:, :, others],
+        send_sem=route_sem.at[0], recv_sem=route_sem.at[1],
+        device_id=(x_up, gy), device_id_type=MESH,
+    ).wait()
+    first = pl.ds(0, CAP)
+    pltpu.make_async_copy(packed.at[:, :, first], landed.at[:, :, first], route_sem.at[2]).wait()
+    copy = pltpu.make_async_copy(landed, owned_out, save_sem.at[2])
+    copy.start()
+    copy.wait()
 
 
 def save(elec, magn, owned, elec_out, magn_out, owned_out, sem):
-    own_r, own_c = pl.ds(TOP, ROWS), pl.ds(LEFT, COLS)
     copies = [
-        pltpu.make_async_copy(elec.at[:, pl.ds(0, NZ), own_r, own_c], elec_out, sem.at[0]),
-        pltpu.make_async_copy(magn.at[:, pl.ds(1, NZ), own_r, own_c], magn_out, sem.at[1]),
+        pltpu.make_async_copy(elec, elec_out, sem.at[0]),
+        pltpu.make_async_copy(magn, magn_out, sem.at[1]),
         pltpu.make_async_copy(owned, owned_out, sem.at[2]),
     ]
     for copy in copies:
@@ -543,18 +584,21 @@
 def body(n_x, n_y, elec, magn, perm, spec, freq, mask, owner):
     hbm = pl.BlockSpec(memory_space=pltpu.HBM)
     vmem = pl.BlockSpec(memory_space=pltpu.VMEM)
+    any_space = pl.BlockSpec(memory_space=pl.ANY)
     buf = pltpu.VMEM
     sem = pltpu.SemaphoreType.DMA
     held = pl.pallas_call(
         functools.partial(kernel, n_x, n_y),
         out_shape=(
-            buf((3, NZ + 1, XROWS, XCOLS), F32),
-            buf((3, NZ + 1, XROWS, XCOLS), F32),
+            buf((3, NZ, ROWS, COLS), F32),
+            buf((3, NZ, ROWS, COLS), F32),
             buf((FREQ, DP, n_x * CAP, COLS), F32),
         ),
         in_specs=[hbm] * 7,
-        out_specs=(vmem, vmem, vmem),
+        out_specs=(any_space,) * 3,
         scratch_shapes=[
+            buf((3, NZ + 1, XROWS, XCOLS), F32),
+            buf((3, NZ + 1, XROWS, XCOLS), F32),
             buf((3, NZ, XROWS, XCOLS), F32),
             buf((FREQ, 2, 3, DP, ROWS, COLS), F32),
             pltpu.SMEM((FREQ,), F32),
@@ -568,17 +612,17 @@
             buf((RADIUS + 1, XROWS, COLS), F32),
             buf((ROWS, COLS), F32),
             buf((FREQ, DP, n_x * CAP, COLS), F32),
+            buf((FREQ, DP, n_x * CAP, COLS), F32),
             buf((2, ROWS, 256), F32), buf((2, XROWS, 256), F32),
             buf((2, len(INNER), 24, COLS), F32), buf((2, len(INNER), 24, COLS), F32),
             buf((2, ROWS, 256), F32), buf((2, XROWS, 256), F32),
             buf((2, len(OUTER), 24, COLS), F32), buf((2, len(OUTER), 24, COLS), F32),
-            buf((2, ROWS, 128), F32), buf((2, XROWS, 128), F32),
-            buf((2, ROWS, COLS), F32), buf((2, ROWS, COLS), F32),
-            sem((13,)), sem((FREQ,)), sem((3, 8)), sem((3, 8)),
-            sem((FREQ, n_x)), sem((FREQ, n_x)),
+            buf((2, 2, 16, 128), F32), buf((2, 2, 32, 128), F32),
+            buf((2, 2, 32, COLS), F32), buf((2, 2, 32, COLS), F32),
+            sem((10,)), sem((3,)), sem((4, 2)), sem((4, 2)), sem((3,)),
         ],
         compiler_params=pltpu.CompilerParams(
-            collective_id=0, has_side_effects=True, vmem_limit_bytes=36 << 20
+            collective_id=0, has_side_effects=True, vmem_limit_bytes=40 << 20
         ),
         name="adjoint",
     )(*[pltpu.with_memory_space_constraint(v, pltpu.HBM) for v in (elec, magn, perm, spec, freq, mask, owner.reshape(8, 128))])

time: 72.2 us -> 65.3 us (0.904)
  Pallas kernels: 71.4 us -> 64.6 us
    pallas_call x1, Pallas kernels: 68 us -> 61.2 us  [body(): pl.pallas_call(functools.partial(kernel, n_x, n_y), out_shape=(buf((3, NZ...]
where the time goes in v3:
time: 65.3 us; the launch traced here: 65.2 us
  Pallas kernels  64.6 us (99%)
    pallas_call x1, Pallas kernels, body(): pl.pallas_call(functools.partial(kernel, n_x, n_y), out_shape=(buf((3, NZ...  61.2 us
    pallas_call x1, Pallas kernels, body(): pl.pallas_call(save, out_shape=(jax.ShapeDtypeStruct((3, NZ, ROWS, COLS),...  3.42 us

profile of v3, /device:TPU:1, one launch (start us, length us, event | category | flops | bytes accessed | tf_op | source)
XLA Modules:
  0.0 65.2 jit_solution(11401200336780312784)
XLA Ops:
  0.6 61.2 %adjoint.1 = (f32[3,16,64,256]{3,2,1,0:T(8,128)S(1)}, f32[3,16,64,256]{3,2,1,0:T(8,128)S(1)}, f32[4,4,128,256]{3,2,1,0:T(8,128)S(1)}) custom-call(f32[3,16,64,256]{3,2,1,0:T(8,128)} %elec_in.1, f32[3,16,64,256]{3,2,1,0:T(8,128)} %magn_in.1, f32[3,16,64,256]{3,2,1,0:T(8,128)} %perm_in.1, f32[4,2,3,4,64,256]{5,4,3,2,1,0:T(8,128)} %spec_in.1, f32[4]{0:T(128)} %freq_hbm.1, ...), custom_call_target="tpu_custom_call" | custom-call | tf_op jit(solution)/shard_map/adjoint/pallas_call | solution.py:590
  61.8 3.4 %save.1 = (f32[3,16,64,256]{3,2,1,0:T(8,128)}, f32[3,16,64,256]{3,2,1,0:T(8,128)}, f32[4,4,128,256]{3,2,1,0:T(8,128)}) custom-call(f32[3,16,64,256]{3,2,1,0:T(8,128)S(1)} %get-tuple-element.6.elec, f32[3,16,64,256]{3,2,1,0:T(8,128)S(1)} %get-tuple-element.7.magn, f32[4,4,128,256]{3,2,1,0:T(8,128)S(1)} %get-tuple-element.8.owned), custom_call_target="tpu_custom_call" | custom-call | tf_op jit(solution)/shard_map/save/pallas_call | solution.py:629

commit v4 on v3

--- a/solution.py
+++ b/solution.py
@@ -52,7 +52,7 @@
     elec_in, magn_in, perm_in, spec_in, freq_hbm, mask_in, owner_hbm,
     elec_out, magn_out, owned_out,
     elec, magn, perm, spec, freq_in, mask, owner_in, trig, early, masked, inverse_norm, picker,
-    fold, plane_out, packed, landed,
+    fold, plane_out, packed,
     ysend_i, yrecv_i, xsend_i, xrecv_i,
     ysend_o, yrecv_o, xsend_o, xrecv_o,
     ysend_m, yrecv_m, xsend_m, xrecv_m,
@@ -190,17 +190,19 @@
         )
         copy.wait()
 
-    def unpack_rows_y(planes, yrecv):
+    def unpack_rows_y(planes, yrecv, wanted):
         def unpack_y(t, carry):
             rows = tile_rows(t)
             there = jnp.where(t == 0, has_down, jnp.where(t == 9, has_up, 1.0))
             for group in range(2):
-                if not planes[5 * group:5 * group + 5]:
+                if not set(planes[5 * group:5 * group + 5]) & set(wanted):
                     continue
                 cols = pl.ds(group * 128, 128)
                 low = yrecv[0, rows, cols] * (there * has_left)
                 high = yrecv[1, rows, cols] * (there * has_right)
                 for i, p in enumerate(planes[5 * group:5 * group + 5]):
+                    if p not in wanted:
+                        continue
                     for kind, c, width, place in PIECES:
                         target = 24 * i + place
                         piece = jnp.where(
@@ -211,7 +213,7 @@
 
         lax.fori_loop(0, XROWS // 8, unpack_y, 0)
 
-    def unpack_rows_x(planes, at, xrecv):
+    def unpack_rows_x(start_q, stop_q, at, xrecv):
         def unpack_x(q, carry):
             p = at(q)
             for side in range(2):
@@ -227,7 +229,7 @@
                         )
             return carry
 
-        lax.fori_loop(0, len(planes), unpack_x, 0)
+        lax.fori_loop(start_q, stop_q, unpack_x, 0)
 
     def ahead_x(tiles, t):
         here = tiles[t]
@@ -371,12 +373,11 @@
     pack_rows_x(OUTER, outer_at, xsend_o)
     pack_rows_y(OUTER, ysend_o)
     finish(0, 0, xrecv_i)
-    unpack_rows_x(INNER, inner_at, xrecv_i)
+    unpack_rows_x(0, 8, inner_at, xrecv_i)
     finish(0, 1, yrecv_i)
-    copies_o = exchange(1, ysend_o, yrecv_o, xsend_o, xrecv_o, TOP, ROWS)
-    for copy in copies_o:
-        copy.start()
-    unpack_rows_y(INNER, yrecv_i)
+    for copy in exchange(1, ysend_o, yrecv_o, xsend_o, xrecv_o, TOP, ROWS):
+        copy.start()
+    unpack_rows_y(INNER, yrecv_i, INNER[:8])
 
     def keep_planes(s, start, stop):
         def keep_plane(p, carry):
@@ -478,6 +479,8 @@
     for copy in loads_s:
         copy.wait()
     send_edges(0)
+    unpack_rows_x(8, 10, inner_at, xrecv_i)
+    unpack_rows_y(INNER, yrecv_i, INNER[8:])
     magnetic(10, 12)
     electric(10, 12)
     magnetic(9, 11)
@@ -531,18 +534,18 @@
             owner = gx ^ k
             theirs = pl.ds(pl.multiple_of(owner * CAP, CAP), CAP)
             pltpu.make_async_remote_copy(
-                src_ref=packed.at[:, p, theirs], dst_ref=landed.at[:, p, mine],
+                src_ref=packed.at[:, p, theirs], dst_ref=owned_out.at[:, p, mine],
                 send_sem=route_sem.at[0], recv_sem=route_sem.at[1],
                 device_id=(owner, gy), device_id_type=MESH,
             ).start()
         pltpu.make_async_copy(
-            packed.at[:, p, mine], landed.at[:, p, mine], route_sem.at[2]
+            packed.at[:, p, mine], owned_out.at[:, p, mine], route_sem.at[2]
         ).start()
 
     finish(1, 0, xrecv_o)
     finish(1, 1, yrecv_o)
-    unpack_rows_x(OUTER, outer_at, xrecv_o)
-    unpack_rows_y(OUTER, yrecv_o)
+    unpack_rows_x(0, len(OUTER), outer_at, xrecv_o)
+    unpack_rows_y(OUTER, yrecv_o, OUTER)
     for s in range(3):
         magnetic(12 - s, NZ)
         magnetic(0, 3 + s)
@@ -558,15 +561,12 @@
         copy.wait()
     others = pl.ds(0, (n_x - 1) * CAP)
     pltpu.make_async_remote_copy(
-        src_ref=packed.at[:, :, others], dst_ref=landed.at[:, :, others],
+        src_ref=packed.at[:, :, others], dst_ref=owned_out.at[:, :, others],
         send_sem=route_sem.at[0], recv_sem=route_sem.at[1],
         device_id=(x_up, gy), device_id_type=MESH,
     ).wait()
     first = pl.ds(0, CAP)
-    pltpu.make_async_copy(packed.at[:, :, first], landed.at[:, :, first], route_sem.at[2]).wait()
-    copy = pltpu.make_async_copy(landed, owned_out, save_sem.at[2])
-    copy.start()
-    copy.wait()
+    pltpu.make_async_copy(packed.at[:, :, first], owned_out.at[:, :, first], route_sem.at[2]).wait()
 
 
 def save(elec, magn, owned, elec_out, magn_out, owned_out, sem):
@@ -612,14 +612,13 @@
             buf((RADIUS + 1, XROWS, COLS), F32),
             buf((ROWS, COLS), F32),
             buf((FREQ, DP, n_x * CAP, COLS), F32),
-            buf((FREQ, DP, n_x * CAP, COLS), F32),
             buf((2, ROWS, 256), F32), buf((2, XROWS, 256), F32),
             buf((2, len(INNER), 24, COLS), F32), buf((2, len(INNER), 24, COLS), F32),
             buf((2, ROWS, 256), F32), buf((2, XROWS, 256), F32),
             buf((2, len(OUTER), 24, COLS), F32), buf((2, len(OUTER), 24, COLS), F32),
             buf((2, 2, 16, 128), F32), buf((2, 2, 32, 128), F32),
             buf((2, 2, 32, COLS), F32), buf((2, 2, 32, COLS), F32),
-            sem((10,)), sem((3,)), sem((4, 2)), sem((4, 2)), sem((3,)),
+            sem((10,)), sem((2,)), sem((4, 2)), sem((4, 2)), sem((3,)),
         ],
         compiler_params=pltpu.CompilerParams(
             collective_id=0, has_side_effects=True, vmem_limit_bytes=40 << 20

time: 65.3 us -> 64.9 us (level)
  no operation moved by 1% of the time
where the time goes in v4:
time: 64.9 us; the launch traced here: 64.8 us
  Pallas kernels  64.2 us (99%)
    pallas_call x1, Pallas kernels, body(): pl.pallas_call(functools.partial(kernel, n_x, n_y), out_shape=(buf((3, NZ...  60.8 us
    pallas_call x1, Pallas kernels, body(): pl.pallas_call(save, out_shape=(jax.ShapeDtypeStruct((3, NZ, ROWS, COLS),...  3.42 us

profile of v4, /device:TPU:1, one launch (start us, length us, event | category | flops | bytes accessed | tf_op | source)
XLA Modules:
  0.0 64.8 jit_solution(2345836803284783416)
XLA Ops:
  0.6 60.8 %adjoint.1 = (f32[3,16,64,256]{3,2,1,0:T(8,128)S(1)}, f32[3,16,64,256]{3,2,1,0:T(8,128)S(1)}, f32[4,4,128,256]{3,2,1,0:T(8,128)S(1)}) custom-call(f32[3,16,64,256]{3,2,1,0:T(8,128)} %elec_in.1, f32[3,16,64,256]{3,2,1,0:T(8,128)} %magn_in.1, f32[3,16,64,256]{3,2,1,0:T(8,128)} %perm_in.1, f32[4,2,3,4,64,256]{5,4,3,2,1,0:T(8,128)} %spec_in.1, f32[4]{0:T(128)} %freq_hbm.1, ...), custom_call_target="tpu_custom_call" | custom-call | tf_op jit(solution)/shard_map/adjoint/pallas_call | solution.py:590
  61.4 3.4 %save.1 = (f32[3,16,64,256]{3,2,1,0:T(8,128)}, f32[3,16,64,256]{3,2,1,0:T(8,128)}, f32[4,4,128,256]{3,2,1,0:T(8,128)}) custom-call(f32[3,16,64,256]{3,2,1,0:T(8,128)S(1)} %get-tuple-element.6.elec, f32[3,16,64,256]{3,2,1,0:T(8,128)S(1)} %get-tuple-element.7.magn, f32[4,4,128,256]{3,2,1,0:T(8,128)S(1)} %get-tuple-element.8.owned), custom_call_target="tpu_custom_call" | custom-call | tf_op jit(solution)/shard_map/save/pallas_call | solution.py:628
